TPU v7x, 128 devices: a whole 4x4x4 slice. The times are simulated.
128 devices in a mesh: dp: 8 (over y_lo, z), tensor: 16 (over x, y_hi, core).
Axes of the slice: x: 4, y: 4 (y_hi: 2, y_lo: 2; y = y_hi * 2 + y_lo), z: 4, core: 2. Of those that a mesh axis runs over, the one named last changes fastest.
Arguments:
- tokens: bfloat16 [1024, 4096], P(('dp', 'tensor')), may hold values from -6 to 6
- out_grad: bfloat16 [1024, 4096], P(('dp', 'tensor')), may hold values from -6 to 6
- gate_blocks: bfloat16 [1792, 128, 128], P('tensor'), may hold values from -0.125 to 0.125
- up_blocks: bfloat16 [1792, 128, 128], P('tensor'), may hold values from -0.125 to 0.125
- down_blocks: bfloat16 [1792, 128, 128], P('tensor'), may hold values from -0.0625 to 0.0625
- gate_index: int32 [16, 112], P('tensor'), may hold values from 0 to 223, as said below
- up_index: int32 [16, 112], P('tensor'), may hold values from 0 to 223, as said below
- down_index: int32 [16, 112], P('tensor'), may hold values from 0 to 223, as said below
- gate_slot: int32 [16, 112], P('tensor'), may hold values from 0 to 135, as said below
- up_slot: int32 [16, 112], P('tensor'), may hold values from 0 to 135, as said below
- down_slot: int32 [16, 112], P('tensor'), may hold values from 0 to 135, as said below
Outputs:
- layer_out: bfloat16 [1024, 4096], P(('dp', 'tensor'))
- token_grad: bfloat16 [1024, 4096], P(('dp', 'tensor'))
- gate_grad: float32 [16, 136, 128, 128], P('tensor', 'dp')
- up_grad: float32 [16, 136, 128, 128], P('tensor', 'dp')
- down_grad: float32 [16, 136, 128, 128], P('tensor', 'dp')
Inputs may be any that keep to these rules, and one draw needn't show every extreme that they name: `gate_index`: each row holds 112 distinct block numbers in increasing order. `up_index`: each row holds 112 distinct block numbers in increasing order. `down_index`: each row holds 112 distinct block numbers in increasing order. `gate_slot`: each row's 112 values are distinct; value v is slot v % 17 of data group v // 17; in every row some data group receives exactly 17 blocks. `up_slot`: each row's 112 values are distinct; value v is slot v % 17 of data group v // 17; in every row some data group receives exactly 17 blocks. `down_slot`: each row's 112 values are distinct; value v is slot v % 17 of data group v // 17; in every row some data group receives exactly 17 blocks.
All inputs are finite; a program needn't handle non-finite values.
Results may differ from a plain program's by a relative error of at most 0.019.
Values may be sent and summed in bfloat16 or wider, within the bound.
A program may use at most 192 MiB of HBM per device.

v0:
```python
import math

import jax
import jax.numpy as jnp
from jax import lax
from jax.sharding import PartitionSpec as P

FF = 14336


def col_sums(picked, blocks, block_cols, out_count):
    product = jnp.einsum("tkd,kde->tke", picked, blocks, preferred_element_type=jnp.float32)
    onehot = (block_cols[:, None] == jnp.arange(out_count, dtype=jnp.int32)[None, :]).astype(
        jnp.float32
    )
    summed = jnp.einsum("tke,kc->tce", product, onehot, precision=lax.Precision.HIGHEST)
    return summed.reshape(summed.shape[0], out_count * blocks.shape[2])


def row_sums(picked, blocks, block_rows, out_count):
    product = jnp.einsum("tke,kde->tkd", picked, blocks, preferred_element_type=jnp.float32)
    onehot = (block_rows[:, None] == jnp.arange(out_count, dtype=jnp.int32)[None, :]).astype(
        jnp.float32
    )
    summed = jnp.einsum("tkd,kr->trd", product, onehot, precision=lax.Precision.HIGHEST)
    return summed.reshape(summed.shape[0], out_count * blocks.shape[1])


def block_terms(picked_left, picked_right, factor):
    return (
        jnp.einsum("tkd,tke->kde", picked_left, picked_right, preferred_element_type=jnp.float32)
        * factor
    )


def owner_buffer(terms, slots, slot_total):
    return jnp.zeros((slot_total,) + terms.shape[1:], jnp.float32).at[slots].set(terms)


def local(
    tokens,
    out_grad,
    gate_blocks,
    up_blocks,
    down_blocks,
    gate_index,
    up_index,
    down_index,
    gate_slot,
    up_slot,
    down_slot,
):
    model_width = tokens.shape[1]
    block_size = gate_blocks.shape[1]
    kept_count = gate_blocks.shape[0]
    group_count = lax.axis_size("dp")
    d_cols = model_width // block_size
    ff_cols = FF // (lax.axis_size("tensor") * block_size)
    capacity = (kept_count + group_count - 1) // group_count + kept_count // (4 * group_count)
    slot_total = group_count * capacity
    gate_ids, up_ids, down_ids = (gate_index[0], up_index[0], down_index[0])
    gate_rows, gate_cols = (gate_ids // ff_cols, gate_ids % ff_cols)
    up_rows, up_cols = (up_ids // ff_cols, up_ids % ff_cols)
    down_rows, down_cols = (down_ids // d_cols, down_ids % d_cols)
    gathered = lax.all_gather(tokens, "tensor", axis=0, tiled=True)
    row_total = gathered.shape[0]
    factor = 1.0 / math.sqrt(row_total * group_count)
    token_blocks = gathered.reshape(row_total, d_cols, block_size)
    tokens_gate = jnp.take(token_blocks, gate_rows, axis=1)
    tokens_up = jnp.take(token_blocks, up_rows, axis=1)
    gate_act = col_sums(tokens_gate, gate_blocks, gate_cols, ff_cols)
    up_act = col_sums(tokens_up, up_blocks, up_cols, ff_cols)
    sigma = jax.nn.sigmoid(gate_act)
    hidden = (gate_act * sigma * up_act).astype(jnp.bfloat16)
    hidden_blocks = hidden.reshape(row_total, ff_cols, block_size)
    hidden_picked = jnp.take(hidden_blocks, down_rows, axis=1)
    layer_out = lax.psum_scatter(
        col_sums(hidden_picked, down_blocks, down_cols, d_cols).astype(jnp.bfloat16),
        "tensor",
        scatter_dimension=0,
        tiled=True,
    )
    cot_rows = lax.all_gather(out_grad, "tensor", axis=0, tiled=True)
    cot_blocks = cot_rows.reshape(row_total, d_cols, block_size)
    cot_picked = jnp.take(cot_blocks, down_cols, axis=1)
    hidden_grad = row_sums(cot_picked, down_blocks, down_rows, ff_cols)
    down_terms = block_terms(hidden_picked, cot_picked, factor)
    gate_pre = (hidden_grad * up_act * sigma * (1.0 + gate_act * (1.0 - sigma))).astype(
        jnp.bfloat16
    )
    up_pre = (hidden_grad * gate_act * sigma).astype(jnp.bfloat16)
    gate_pre_picked = jnp.take(gate_pre.reshape(row_total, ff_cols, block_size), gate_cols, axis=1)
    up_pre_picked = jnp.take(up_pre.reshape(row_total, ff_cols, block_size), up_cols, axis=1)
    first_part = row_sums(gate_pre_picked, gate_blocks, gate_rows, d_cols)
    token_grad = lax.psum_scatter(
        (first_part + row_sums(up_pre_picked, up_blocks, up_rows, d_cols)).astype(jnp.bfloat16),
        "tensor",
        scatter_dimension=0,
        tiled=True,
    )
    gate_terms = block_terms(tokens_gate, gate_pre_picked, factor)
    up_terms = block_terms(tokens_up, up_pre_picked, factor)
    gate_out, up_out, down_out = (
        lax.psum_scatter(
            owner_buffer(gate_terms, gate_slot[0], slot_total).astype(jnp.bfloat16),
            "dp",
            scatter_dimension=0,
            tiled=True,
        ).astype(jnp.float32),
        lax.psum_scatter(
            owner_buffer(up_terms, up_slot[0], slot_total).astype(jnp.bfloat16),
            "dp",
            scatter_dimension=0,
            tiled=True,
        ).astype(jnp.float32),
        lax.psum_scatter(
            owner_buffer(down_terms, down_slot[0], slot_total).astype(jnp.bfloat16),
            "dp",
            scatter_dimension=0,
            tiled=True,
        ).astype(jnp.float32),
    )
    return (layer_out, token_grad, gate_out[None], up_out[None], down_out[None])


def solution(mesh):
    in_specs = (
        P(("dp", "tensor"), None),
        P(("dp", "tensor"), None),
        P("tensor", None, None),
        P("tensor", None, None),
        P("tensor", None, None),
        P("tensor", None),
        P("tensor", None),
        P("tensor", None),
        P("tensor", None),
        P("tensor", None),
        P("tensor", None),
    )
    out_specs = (
        P(("dp", "tensor"), None),
        P(("dp", "tensor"), None),
        P("tensor", "dp", None, None),
        P("tensor", "dp", None, None),
        P("tensor", "dp", None, None),
    )
    return jax.shard_map(local, mesh=mesh, in_specs=in_specs, out_specs=out_specs, check_vma=False)
```

profile of v0, /device:TPU:0, one launch (start us, length us, event | category | flops | bytes accessed | tf_op | source)
XLA Modules:
  0.0 492.0 jit_solution(15242392791960012088)
XLA Ops:
  11.5 46.3 %all-gather.3.cloned.1.call-done = bf16[128,4096]{1,0:T(8,128)(2,1)} async-done(((bf16[8,4096]{1,0:T(8,128)(2,1)}), bf16[128,4096]{1,0:T(8,128)(2,1)}) %all-gather.3.cloned.1.call-update) | async-done | bytes 1048592 | tf_op jit(solution)/shard_map/all_gather | solution.py:65
  60.1 2.9 gather_fusion
  65.9 4.4 fusion.36
  70.2 6.6 %fusion.8 = f32[7,128,128]{2,0,1:T(8,128)S(1)} fusion(f32[128,112,128]{2,0,1:T(8,128)S(1)} %fusion.36, s32[112]{0:T(128)S(1)} %get-tuple-element.10), kind=kOutput, calls=%fused_computation.17 | convolution fusion | flops 154141456 | bytes 7799232 | tf_op jit(solution)/shard_map/tke,kc->tce/dot_general | solution.py:16
  76.8 27.2 %all-gather.5.cloned.1.call-done = bf16[128,4096]{1,0:T(8,128)(2,1)} async-done(((bf16[8,4096]{1,0:T(8,128)(2,1)}), bf16[128,4096]{1,0:T(8,128)(2,1)}) %all-gather.5.cloned.1.call-update) | async-done | bytes 1048592 | tf_op jit(solution)/shard_map/all_gather | solution.py:83
  106.5 4.3 fusion.33
  110.8 6.6 %fusion.10 = f32[7,128,128]{2,0,1:T(8,128)S(1)} fusion(f32[128,112,128]{2,0,1:T(8,128)S(1)} %fusion.33, s32[112]{0:T(128)S(1)} %get-tuple-element.8), kind=kOutput, calls=%fused_computation.19 | convolution fusion | flops 154141456 | bytes 7799232 | tf_op jit(solution)/shard_map/tke,kc->tce/dot_general | solution.py:16
  117.4 2.9 gather_fusion.3
  120.3 5.9 %fusion.42 = f32[128,112,128]{2,0,1:T(8,128)S(1)} fusion(bf16[112,128,128]{2,1,0:T(8,128)(2,1)} %param.19, bf16[112,128,128]{2,1,0:T(8,128)(2,1)} %gather_fusion.3, pred[112]{0:T(512)(128)(4,1)S(1)} %get-tuple-element.11), kind=kOutput, calls=%fused_computation.54 | convolution fusion | flops 471597056 | bytes 14680176 | tf_op jit(solution)/shard_map/tke,kde->tkd/dot_general | solution.py:21
  126.2 7.0 %fusion.4 = f32[7,128,128]{2,0,1:T(8,128)S(1)} fusion(f32[128,112,128]{2,0,1:T(8,128)S(1)} %fusion.42, s32[112]{0:T(128)S(1)} %get-tuple-element.23), kind=kOutput, calls=%fused_computation.13 | convolution fusion | flops 154141456 | bytes 7799232 | tf_op jit(solution)/shard_map/tkd,kr->trd/dot_general | solution.py:25
  133.5 2.9 gather_fusion.5
  136.4 7.7 %broadcast_multiply_fusion.1 = f32[112,128,128]{2,1,0:T(8,128)} fusion(bf16[112,128,128]{2,1,0:T(8,128)(2,1)} %gather_fusion.1, pred[112]{0:T(512)(128)(4,1)S(1)} %get-tuple-element.26, bf16[112,128,128]{2,1,0:T(8,128)(2,1)} %gather_fusion.5, pred[112]{0:T(512)(128)(4,1)S(1)} %get-tuple-element.9), kind=kOutput, calls=%fused_computation.43 | convolution fusion | flops 475267072 | bytes 14680288 | tf_op jit(solution)/shard_map/tkd,tke->kde/dot_general | solution.py:31
  144.1 4.6 broadcast.208.clone.1
  148.7 20.7 %scatter_fusion.1 = f32[136,128,128]{2,1,0:T(8,128)} fusion(f32[136,128,128]{2,1,0:T(8,128)} %broadcast.208.clone.1, s32[112]{0:T(128)S(1)} %fusion.99, f32[112,128,128]{2,1,0:T(8,128)} %broadcast_multiply_fusion.1), kind=kCustom, calls=%fused_computation.7 | custom fusion | bytes 22020544 | tf_op jit(solution)/shard_map/scatter | solution.py:37
  169.3 6.6 %convert_element_type.58 = bf16[136,128,128]{2,1,0:T(8,128)(2,1)} convert(f32[136,128,128]{2,1,0:T(8,128)} %scatter_fusion.1) | non-fusion elementwise | flops 2228224 | bytes 13369344 | tf_op jit(solution)/shard_map/convert_element_type | solution.py:111
  176.6 2.9 gather_fusion.4
  179.5 7.7 %broadcast_multiply_fusion.2 = f32[112,128,128]{2,1,0:T(8,128)} fusion(bf16[112,128,128]{2,1,0:T(8,128)(2,1)} %gather_fusion, pred[112]{0:T(512)(128)(4,1)S(1)} %get-tuple-element.24, bf16[112,128,128]{2,1,0:T(8,128)(2,1)} %gather_fusion.4, pred[112]{0:T(512)(128)(4,1)S(1)} %get-tuple-element.7), kind=kOutput, calls=%fused_computation.44 | convolution fusion | flops 475267072 | bytes 14680288 | tf_op jit(solution)/shard_map/tkd,tke->kde/dot_general | solution.py:31
  187.2 4.6 broadcast.208.clone
  191.8 20.8 %scatter_fusion = f32[136,128,128]{2,1,0:T(8,128)} fusion(f32[136,128,128]{2,1,0:T(8,128)} %broadcast.208.clone, s32[112]{0:T(128)S(1)} %fusion.98, f32[112,128,128]{2,1,0:T(8,128)} %broadcast_multiply_fusion.2), kind=kCustom, calls=%fused_computation.6 | custom fusion | bytes 22020544 | tf_op jit(solution)/shard_map/scatter | solution.py:37
  212.5 6.8 %convert_element_type.57 = bf16[136,128,128]{2,1,0:T(8,128)(2,1)} convert(f32[136,128,128]{2,1,0:T(8,128)} %scatter_fusion) | non-fusion elementwise | flops 2228224 | bytes 13369344 | tf_op jit(solution)/shard_map/convert_element_type | solution.py:105
  222.8 7.8 %broadcast_multiply_fusion = f32[112,128,128]{2,1,0:T(8,128)} fusion(bf16[112,128,128]{2,1,0:T(8,128)(2,1)} %gather_fusion.2, pred[112]{0:T(512)(128)(4,1)S(1)} %get-tuple-element.22, bf16[112,128,128]{2,1,0:T(8,128)(2,1)} %gather_fusion.3, pred[112]{0:T(512)(128)(4,1)S(1)} %get-tuple-element.11), kind=kOutput, calls=%fused_computation.42 | convolution fusion | flops 475267072 | bytes 14680288 | tf_op jit(solution)/shard_map/tkd,tke->kde/dot_general | solution.py:31
  230.6 4.6 broadcast.208.clone.2
  235.1 20.7 %scatter_fusion.2 = f32[136,128,128]{2,1,0:T(8,128)} fusion(f32[136,128,128]{2,1,0:T(8,128)} %broadcast.208.clone.2, s32[112]{0:T(128)S(1)} %fusion.100, f32[112,128,128]{2,1,0:T(8,128)} %broadcast_multiply_fusion), kind=kCustom, calls=%fused_computation.8 | custom fusion | bytes 22020544 | tf_op jit(solution)/shard_map/scatter | solution.py:37
  255.8 6.8 %convert_element_type.59 = bf16[136,128,128]{2,1,0:T(8,128)(2,1)} convert(f32[136,128,128]{2,1,0:T(8,128)} %scatter_fusion.2) | non-fusion elementwise | flops 2228224 | bytes 13369344 | tf_op jit(solution)/shard_map/convert_element_type | solution.py:117
  263.0 6.0 %fusion.48 = f32[128,112,128]{2,0,1:T(8,128)S(1)} fusion(bf16[112,128,128]{2,1,0:T(8,128)(2,1)} %param.18, bf16[112,128,128]{2,1,0:T(8,128)(2,1)} %gather_fusion.5, pred[112]{0:T(512)(128)(4,1)S(1)} %get-tuple-element.9), kind=kOutput, calls=%fused_computation.56 | convolution fusion | flops 471597056 | bytes 14680176 | tf_op jit(solution)/shard_map/tke,kde->tkd/dot_general | solution.py:21
  269.0 6.8 %fusion = f32[32,128,128]{2,0,1:T(8,128)S(1)} fusion(f32[128,112,128]{2,0,1:T(8,128)S(1)} %fusion.48, s32[112]{0:T(128)S(1)} %get-tuple-element.27), kind=kOutput, calls=%fused_computation.9 | convolution fusion | flops 704646656 | bytes 9437632 | tf_op jit(solution)/shard_map/tkd,kr->trd/dot_general | solution.py:25
  278.5 7.1 %add_convert_fusion = bf16[32,128,128]{2,0,1:T(8,128)(2,1)S(1)} fusion(f32[32,128,128]{2,0,1:T(8,128)S(1)} %fusion, f32[128,112,128]{2,0,1:T(8,128)S(1)} %fusion.45, s32[112]{0:T(128)S(1)} %get-tuple-element.25), kind=kOutput, calls=%fused_computation.57 | convolution fusion | flops 705695232 | bytes 10486208 | tf_op jit(solution)/shard_map/tkd,kr->trd/dot_general | solution.py:25
  287.1 4.3 fusion.39
  291.4 6.8 %fusion.65 = bf16[32,128,128]{2,0,1:T(8,128)(2,1)S(1)} fusion(f32[128,112,128]{2,0,1:T(8,128)S(1)} %fusion.39, s32[112]{0:T(128)S(1)} %get-tuple-element.12), kind=kOutput, calls=%fused_computation.58 | convolution fusion | flops 705170944 | bytes 8389056 | tf_op jit(solution)/shard_map/tke,kc->tce/dot_general | solution.py:16
  304.0 40.3 %reduce-scatter.14.cloned.1.call-done = bf16[17,128,128]{2,1,0:T(8,128)(2,1)} async-done(((bf16[136,128,128]{2,1,0:T(8,128)(2,1)}), bf16[17,128,128]{2,1,0:T(8,128)(2,1)}) %reduce-scatter.14.cloned.1.call-update) | async-done | bytes 557072 | tf_op jit(solution)/shard_map/reduce_scatter | solution.py:116
  346.5 67.5 %reduce-scatter.8.cloned.1.call-done = bf16[8,4096]{1,0:T(8,128)(2,1)} async-done(((bf16[128,4096]{1,0:T(8,128)(2,1)}), bf16[8,4096]{1,0:T(8,128)(2,1)}) %reduce-scatter.8.cloned.1.call-update) | async-done | bytes 65552 | tf_op jit(solution)/shard_map/reduce_scatter | solution.py:95
  414.0 70.7 %reduce-scatter.6.cloned.1.call-done = bf16[8,4096]{1,0:T(8,128)(2,1)} async-done(((bf16[128,4096]{1,0:T(8,128)(2,1)}), bf16[8,4096]{1,0:T(8,128)(2,1)}) %reduce-scatter.6.cloned.1.call-update) | async-done | bytes 65552 | tf_op jit(solution)/shard_map/reduce_scatter | solution.py:77
  (55 shorter events, 28.7 us)
Async XLA Ops:
  7.2 50.7 %all-gather.3.cloned.1.call-start = ((), (), s32[]{:S(2)}) async-start(), calls=%async_computation.5 | async-start | bytes 1114112 | tf_op jit(solution)/shard_map/all_gather | solution.py:65
  7.9 96.1 %all-gather.5.cloned.1.call-start = ((), (), s32[]{:S(2)}) async-start(), calls=%async_computation.7 | async-start | bytes 1114112 | tf_op jit(solution)/shard_map/all_gather | solution.py:83
  8.6 291.1 %reduce-scatter.12.cloned.1.call-start = ((), (), s32[]{:S(2)}) async-start(), calls=%async_computation.10 | async-start | bytes 5013504 | tf_op jit(solution)/shard_map/reduce_scatter | solution.py:110
  176.0 0.7 copy-start.2
  176.0 125.9 %reduce-scatter.10.cloned.1.call-start = ((), (), s32[]{:S(2)}) async-start(), calls=%async_computation.9 | async-start | bytes 5013504 | tf_op jit(solution)/shard_map/reduce_scatter | solution.py:104
  219.3 0.7 copy-start.3
  219.3 125.0 %reduce-scatter.14.cloned.1.call-start = ((), (), s32[]{:S(2)}) async-start(), calls=%async_computation.11 | async-start | bytes 5013504 | tf_op jit(solution)/shard_map/reduce_scatter | solution.py:116
  262.7 151.3 %reduce-scatter.8.cloned.1.call-start = ((), (), s32[]{:S(2)}) async-start(), calls=%async_computation.8 | async-start | bytes 1114112 | tf_op jit(solution)/shard_map/reduce_scatter | solution.py:95
  268.9 6.8 %copy-start = (bf16[112,128,128]{2,1,0:T(8,128)(2,1)S(1)}, bf16[112,128,128]{2,1,0:T(8,128)(2,1)}, u32[]{:S(2)}) copy-start(bf16[112,128,128]{2,1,0:T(8,128)(2,1)} %gather_fusion.4) | copy-start | bytes 11010052
  268.9 6.8 %copy-start.1 = (bf16[112,128,128]{2,1,0:T(8,128)(2,1)S(1)}, bf16[112,128,128]{2,1,0:T(8,128)(2,1)}, u32[]{:S(2)}) copy-start(bf16[112,128,128]{2,1,0:T(8,128)(2,1)} %param.17) | copy-start | bytes 11010052
  287.0 197.7 %reduce-scatter.6.cloned.1.call-start = ((), (), s32[]{:S(2)}) async-start(), calls=%async_computation.6 | async-start | bytes 1114112 | tf_op jit(solution)/shard_map/reduce_scatter | solution.py:77
Sparse Core Ops, SparseCore 0:
  10.4 47.3 all-gather.2
  60.2 43.7 all-gather.4
  176.1 54.7 reduce-scatter.11
  233.1 54.3 reduce-scatter.9
  289.8 54.4 reduce-scatter.13
  348.6 65.3 reduce-scatter.7
  418.8 65.8 reduce-scatter.5
where the time goes:
time: 501 us; the launch traced here: 492 us
  waiting for transfers between devices  253 us (50%)
  local copies, waits for them, and re-layouts  102 us (20%)
  matrix products  91.6 us (18%)
  other arithmetic  29.8 us (6%)
  between operations  14.8 us (3%)
    reduce_scatter x1, waiting for transfers between devices, local(): lax.psum_scatter(col_sums(hidden_picked, down_blocks, down_cols, d_cols)....  70.7 us
    reduce_scatter x1, waiting for transfers between devices, local(): lax.psum_scatter((first_part + row_sums(up_pre_picked, up_blocks, up_rows...  67.5 us
    scatter x3, local copies, waits for them, and re-layouts, owner_buffer(): jnp.zeros((slot_total,) + terms.shape[1:], jnp.float32).at[slots].set(terms)  62.1 us
    all_gather x1, waiting for transfers between devices, local(): gathered = lax.all_gather(tokens, 'tensor', axis=0, tiled=True)  46.3 us
    reduce_scatter x1, waiting for transfers between devices, local(): lax.psum_scatter(owner_buffer(down_terms, down_slot[0], slot_total).astyp...  40.3 us
    all_gather x1, waiting for transfers between devices, local(): cot_rows = lax.all_gather(out_grad, 'tensor', axis=0, tiled=True)  27.2 us
    dot_general x3, matrix products, block_terms(): jnp.einsum('tkd,tke->kde', picked_left, picked_right, preferred_element_t...  23.2 us
    dot_general x3, matrix products, row_sums(): jnp.einsum('tkd,kr->trd', product, onehot, precision=lax.Precision.HIGHEST)  20.9 us
  transfers between devices with their start and end apart: 7, of which 5 were waited for; matrix products, arithmetic and copies ran while one was open for 31% of the time, Pallas kernels for 0%

commit v1 on v0

v1 whole, which is shorter than its diff:
```python
import functools
import math

import jax
import jax.numpy as jnp
from jax import lax
from jax.experimental import pallas as pl
from jax.experimental.pallas import tpu as pltpu
from jax.sharding import PartitionSpec as P

MESH = pl.DeviceIdType.MESH
D = 4096
BLK = 128
DC = 32
FC = 7
FDEV = 896
KB = 112
NBLK = 224
CAP = 17
TOK = 1024
F32 = jnp.float32
BF16 = jnp.bfloat16

THIRDS = ((0, 6, 11), (11, 17, 22), (22, 27, 32))
ORDERS = (("x", "y", "z"), ("y", "z", "x"), ("z", "x", "y"))


def kernel_body(
    tab,
    tok_ref,
    cot_ref,
    gb_ref,
    ub_ref,
    db_ref,
    lo_ref,
    tg_ref,
    gg_ref,
    ug_ref,
    dg_ref,
    buf,
    wgu,
    wd,
    stage,
    hid,
    gpre,
    part,
    got1,
    got2,
    mid,
    got3,
    ld_sem,
    ag_send,
    ag_recv,
    sib_send,
    sib_recv,
    rs_send,
    rs_recv,
):
    dp = lax.axis_index("dp")
    tp = lax.axis_index("tensor")
    ylo, z = dp // 4, dp % 4
    x, yhi, core = tp // 4, (tp // 2) % 2, tp % 2
    y = yhi * 2 + ylo
    here = {"x": x, "y": y, "z": z}

    def device(at, c):
        return (
            (at["y"] % 2) * 4 + at["z"],
            at["x"] * 4 + (at["y"] // 2) * 2 + c,
        )

    def moved(axis, step):
        at = dict(here)
        at[axis] = (here[axis] + step) % 4
        return at

    right = {a: device(moved(a, 1), core) for a in "xyz"}
    left = {a: device(moved(a, 3), core) for a in "xyz"}
    far = {a: device(moved(a, 2), core) for a in "xy"}
    sibling = device(here, 1 - core)

    barrier = pltpu.get_barrier_semaphore()
    partners = list(right.values()) + list(left.values()) + list(far.values()) + [sibling]
    for other in partners:
        pl.semaphore_signal(barrier, inc=1, device_id=other, device_id_type=MESH)
    pl.semaphore_wait(barrier, len(partners))

    def region(q, third, phase, along, lo, hi):
        axes = ORDERS[third]
        idx = []
        for a in ("z", "y", "x"):
            if a in axes[:phase]:
                idx.append(slice(None))
            elif a == axes[phase]:
                idx.append(along)
            else:
                idx.append(here[a])
        return buf.at[(q, pl.ds(lo, hi - lo), *idx, core)]

    def ag_copy(q, third, phase, k):
        lo, mid_col, hi = THIRDS[third]
        axis = ORDERS[third][phase]
        own = here[axis]
        along, cols, to = (
            (own, (lo, mid_col), right),
            (own, (mid_col, hi), left),
            (own, (mid_col, hi), right),
            (own, (lo, mid_col), left),
            ((own + 3) % 4, (lo, mid_col), right),
            ((own + 1) % 4, (mid_col, hi), left),
        )[k]
        ref = region(q, third, phase, along, *cols)
        return pltpu.make_async_remote_copy(
            src_ref=ref,
            dst_ref=ref,
            send_sem=ag_send.at[q, third, phase, k],
            recv_sem=ag_recv.at[q, third, phase, k],
            device_id=to[axis],
            device_id_type=MESH,
        )

    def sib_copy(q, third, k):
        lo, _, hi = THIRDS[third]
        axis = ORDERS[third][2]
        ref = region(q, third, 2, (here[axis] + k) % 4, lo, hi)
        return pltpu.make_async_remote_copy(
            src_ref=ref,
            dst_ref=ref,
            send_sem=sib_send.at[q, third, k],
            recv_sem=sib_recv.at[q, third, k],
            device_id=sibling,
            device_id_type=MESH,
        )

    def ag_start(q, phase):
        for k in range(4):
            for third in range(3):
                ag_copy(q, third, phase, k).start()

    def ag_forward(q, phase):
        for third in range(3):
            ag_copy(q, third, phase, 0).wait_recv()
            ag_copy(q, third, phase, 4).start()
            ag_copy(q, third, phase, 1).wait_recv()
            ag_copy(q, third, phase, 5).start()

    def ag_direct(q, phase):
        for third in range(3):
            ag_copy(q, third, phase, 2).wait_recv()
            ag_copy(q, third, phase, 3).wait_recv()

    def ag_far(q, phase):
        for third in range(3):
            ag_copy(q, third, phase, 4).wait_recv()
            ag_copy(q, third, phase, 5).wait_recv()

    def sib_start(q, k):
        for third in range(3):
            sib_copy(q, third, k).start()

    def sib_wait(q):
        for third in range(3):
            for k in range(4):
                sib_copy(q, third, k).wait_recv()

    def ag_finish(q):
        for third in range(3):
            for phase in range(3):
                for k in range(6):
                    ag_copy(q, third, phase, k).wait_send()
            for k in range(4):
                sib_copy(q, third, k).wait_send()

    def load(src):
        return pltpu.make_async_copy(src, stage.at[pl.ds(0, KB)], ld_sem)

    def spread_cols(base, side):
        @pl.loop(0, DC)
        def _(r):
            for c in range(FC):
                rows = pl.ds(pl.multiple_of(r * BLK, BLK), BLK)
                wgu[rows, pl.ds((2 * c + side) * BLK, BLK)] = stage[tab[base + r * FC + c]]

    def spread_rows(base):
        @pl.loop(0, FC)
        def _(r):
            for c in range(DC):
                rows = pl.ds(pl.multiple_of(r * BLK, BLK), BLK)
                wd[rows, pl.ds(c * BLK, BLK)] = stage[tab[base + r * DC + c]]

    for j in range(DC):
        cols = pl.ds(j * BLK, BLK)
        buf[0, j, z, y, x, core] = tok_ref[:, cols]
        buf[1, j, z, y, x, core] = cot_ref[:, cols]
    ag_start(0, 0)
    ag_start(1, 0)
    load(gb_ref).start()
    stage[KB] = jnp.zeros((BLK, BLK), BF16)
    ag_forward(0, 0)
    ag_direct(0, 0)
    ag_far(0, 0)
    ag_start(0, 1)
    ag_forward(1, 0)
    ag_direct(1, 0)
    ag_far(1, 0)
    ag_start(1, 1)
    ag_forward(0, 1)
    ag_direct(0, 1)
    ag_far(0, 1)
    ag_start(0, 2)
    sib_start(0, 0)
    ag_forward(1, 1)
    ag_direct(1, 1)
    ag_far(1, 1)
    load(gb_ref).wait()
    spread_cols(0, 0)
    load(ub_ref).start()
    ag_forward(0, 2)
    ag_start(1, 2)
    sib_start(1, 0)
    load(ub_ref).wait()
    spread_cols(NBLK, 1)
    load(db_ref).start()
    ag_direct(0, 2)
    sib_start(0, 1)
    sib_start(0, 3)
    load(db_ref).wait()
    spread_rows(2 * NBLK)
    ag_far(0, 2)
    sib_start(0, 2)
    sib_wait(0)

    flat = buf.reshape(2, DC, TOK, BLK)
    MT = 256

    def rows_of(q, rows):
        return jnp.concatenate([flat[q, j, rows, :] for j in range(DC)], axis=1)

    def forward_cols(c):
        @pl.loop(0, TOK // MT)
        def _(m):
            rows = pl.ds(pl.multiple_of(m * MT, MT), MT)
            both = jnp.dot(
                rows_of(0, rows), wgu[:, pl.ds(c * 2 * BLK, 2 * BLK)], preferred_element_type=F32
            )
            gate, up = both[:, :BLK], both[:, BLK:]
            sigma = 1.0 / (1.0 + jnp.exp(-gate))
            swish = gate * sigma
            hid[c, rows, :] = (swish * up).astype(BF16)
            gpre[2 * c, rows, :] = (
                up * sigma * (1.0 + gate * (1.0 - sigma))
            ).astype(BF16)
            gpre[2 * c + 1, rows, :] = swish.astype(BF16)

    forward_cols(0)
    ag_forward(1, 2)
    forward_cols(1)
    ag_direct(1, 2)
    sib_start(1, 1)
    sib_start(1, 3)
    for c in range(2, FC):
        forward_cols(c)
    ag_far(1, 2)
    sib_start(1, 2)

    def own_rows(ref):
        runs = []
        for h in range(2):
            rows = pl.ds(pl.multiple_of((z * 4 + h * 2 + ylo) * 64, 64), 64)
            runs.append(jnp.concatenate([ref[j, rows, :] for j in range(ref.shape[0])], axis=1))
        return jnp.concatenate(runs, axis=0)

    def partial_out(o, left_side, weights, contract):
        width = 512

        @pl.loop(0, D // width)
        def _(n):
            cols = pl.ds(pl.multiple_of(n * width, width), width)
            w = weights[:, cols] if contract == 0 else weights[cols, :]
            term = lax.dot_general(
                left_side, w, (((1,), (contract,)), ((), ())), preferred_element_type=F32
            ).astype(BF16)
            part[o, :, :, :, :, cols] = term.reshape(2, 4, 2, 8, width)

    def rs_copy(o, k):
        if k == 0:
            src, dst, to = part.at[o, :, :, 1 - core], got1.at[o], sibling
        elif k < 4:
            at = moved("x", k)
            src, dst, to = part.at[o, :, at["x"], core], got2.at[o, k - 1], device(at, core)
        else:
            src, dst, to = mid.at[o, 1 - yhi], got3.at[o], far["y"]
        return pltpu.make_async_remote_copy(
            src_ref=src,
            dst_ref=dst,
            send_sem=rs_send.at[o, k],
            recv_sem=rs_recv.at[o, k],
            device_id=to,
            device_id_type=MESH,
        )

    def rs_one(o):
        rs_copy(o, 0).start()

    def rs_two(o):
        rs_copy(o, 0).wait_recv()
        for h in range(2):
            for w in range(4):
                part[o, h, w, core] = (
                    part[o, h, w, core].astype(F32) + got1[o, h, w].astype(F32)
                ).astype(BF16)
        for k in (2, 1, 3):
            rs_copy(o, k).start()

    def rs_three(o):
        for k in range(1, 4):
            rs_copy(o, k).wait_recv()
        for h in range(2):
            total = part[o, h, x, core].astype(F32)
            for k in range(3):
                total = total + got2[o, k, h].astype(F32)
            mid[o, h] = total.astype(BF16)
        rs_copy(o, 4).start()

    def rs_four(o, out):
        rs_copy(o, 4).wait_recv()
        out[...] = (mid[o, yhi].astype(F32) + got3[o].astype(F32)).astype(BF16)
        for k in range(5):
            rs_copy(o, k).wait_send()

    partial_out(0, own_rows(hid), wd, 0)
    rs_one(0)
    sib_wait(1)

    def backward_cols(start, width):
        @pl.loop(0, TOK // MT)
        def _(m):
            rows = pl.ds(pl.multiple_of(m * MT, MT), MT)
            grad = lax.dot_general(
                rows_of(1, rows),
                wd[pl.ds(start * BLK, width * BLK), :],
                (((1,), (1,)), ((), ())),
                preferred_element_type=F32,
            )
            for j in range(width):
                piece = grad[:, j * BLK : (j + 1) * BLK]
                for side in range(2):
                    k = 2 * (start + j) + side
                    gpre[k, rows, :] = (gpre[k, rows, :].astype(F32) * piece).astype(BF16)

    backward_cols(0, 2)
    rs_two(0)
    backward_cols(2, 2)
    backward_cols(4, 2)
    rs_three(0)
    backward_cols(6, 1)
    partial_out(1, own_rows(gpre), wgu, 1)
    rs_one(1)

    factor = 1.0 / math.sqrt(TOK)

    def grads(base, left, right, out):
        @pl.loop(0, CAP)
        def _(v):
            weight = tab[base + 2 * CAP + v].astype(F32) * factor
            a = left(tab[base + v])
            b = right(tab[base + CAP + v])
            out[v] = (
                lax.dot_general(a, b, (((0,), (0,)), ((), ())), preferred_element_type=F32) * weight
            )

    def token_block(row):
        return buf[0, row].reshape(TOK, BLK)

    def cot_block(col):
        return buf[1, col].reshape(TOK, BLK)

    slots = 3 * NBLK
    rs_two(1)
    grads(slots, token_block, lambda col: gpre[2 * col], gg_ref)
    rs_three(1)
    rs_four(0, lo_ref)
    grads(slots + 3 * CAP, token_block, lambda col: gpre[2 * col + 1], ug_ref)
    rs_four(1, tg_ref)
    grads(slots + 6 * CAP, lambda row: hid[row], cot_block, dg_ref)
    ag_finish(0)
    ag_finish(1)


def tables(ids, slots, cols, me):
    match = ids[None, :] == jnp.arange(NBLK, dtype=jnp.int32)[:, None]
    order = jnp.arange(KB, dtype=jnp.int32)[None, :]
    where = KB + jnp.sum(jnp.where(match, order - KB, 0), axis=1)
    mine = slots[None, :] == me * CAP + jnp.arange(CAP, dtype=jnp.int32)[:, None]
    row = jnp.sum(jnp.where(mine, ids[None, :] // cols, 0), axis=1)
    col = jnp.sum(jnp.where(mine, ids[None, :] % cols, 0), axis=1)
    full = jnp.sum(mine.astype(jnp.int32), axis=1)
    return where, jnp.concatenate([row, col, full])


def local(
    tokens,
    out_grad,
    gate_blocks,
    up_blocks,
    down_blocks,
    gate_index,
    up_index,
    down_index,
    gate_slot,
    up_slot,
    down_slot,
):
    me = lax.axis_index("dp")
    parts = [
        tables(gate_index[0], gate_slot[0], FC, me),
        tables(up_index[0], up_slot[0], FC, me),
        tables(down_index[0], down_slot[0], DC, me),
    ]
    tab = jnp.concatenate([p[0] for p in parts] + [p[1] for p in parts])
    vmem = pl.BlockSpec(memory_space=pltpu.VMEM)
    hbm = pl.BlockSpec(memory_space=pl.ANY)
    rows = jax.ShapeDtypeStruct((8, D), BF16)
    owned = jax.ShapeDtypeStruct((CAP, BLK, BLK), F32)
    lo, tg, gg, ug, dg = pl.pallas_call(
        kernel_body,
        out_shape=(rows, rows, owned, owned, owned),
        in_specs=[pl.BlockSpec(memory_space=pltpu.SMEM), vmem, vmem, hbm, hbm, hbm],
        out_specs=(vmem,) * 5,
        scratch_shapes=[
            pltpu.VMEM((2, DC, 4, 4, 4, 2, 8, BLK), BF16),
            pltpu.VMEM((D, 2 * FDEV), BF16),
            pltpu.VMEM((FDEV, D), BF16),
            pltpu.VMEM((KB + 1, BLK, BLK), BF16),
            pltpu.VMEM((FC, TOK, BLK), BF16),
            pltpu.VMEM((2 * FC, TOK, BLK), BF16),
            pltpu.VMEM((2, 2, 4, 2, 8, D), BF16),
            pltpu.VMEM((2, 2, 4, 8, D), BF16),
            pltpu.VMEM((2, 3, 2, 8, D), BF16),
            pltpu.VMEM((2, 2, 8, D), BF16),
            pltpu.VMEM((2, 8, D), BF16),
            pltpu.SemaphoreType.DMA,
            pltpu.SemaphoreType.DMA((2, 3, 3, 6)),
            pltpu.SemaphoreType.DMA((2, 3, 3, 6)),
            pltpu.SemaphoreType.DMA((2, 3, 4)),
            pltpu.SemaphoreType.DMA((2, 3, 4)),
            pltpu.SemaphoreType.DMA((2, 5)),
            pltpu.SemaphoreType.DMA((2, 5)),
        ],
        compiler_params=pltpu.CompilerParams(
            collective_id=0, has_side_effects=True, vmem_limit_bytes=61 * 1024 * 1024
        ),
    )(tab, tokens, out_grad, gate_blocks, up_blocks, down_blocks)
    return lo, tg, gg[None], ug[None], dg[None]


def solution(mesh):
    in_specs = (
        P(("dp", "tensor"), None),
        P(("dp", "tensor"), None),
        P("tensor", None, None),
        P("tensor", None, None),
        P("tensor", None, None),
        P("tensor", None),
        P("tensor", None),
        P("tensor", None),
        P("tensor", None),
        P("tensor", None),
        P("tensor", None),
    )
    out_specs = (
        P(("dp", "tensor"), None),
        P(("dp", "tensor"), None),
        P("tensor", "dp", None, None),
        P("tensor", "dp", None, None),
        P("tensor", "dp", None, None),
    )
    return jax.shard_map(local, mesh=mesh, in_specs=in_specs, out_specs=out_specs, check_vma=False)
```

time: 501 us -> 126 us (0.25); the launches traced: 492 us -> 125 us
  waiting for transfers between devices: 253 us -> 0 us
  Pallas kernels: 0 us -> 112 us
  local copies, waits for them, and re-layouts: 102 us -> 8.7 us
  matrix products: 91.6 us -> 0 us
  other arithmetic: 29.8 us -> 3.27 us
  between operations: 14.8 us -> 0.68 us
    reduce_scatter x5 -> x0, waiting for transfers between devices: 179 us -> none  [the longest x1 70.7 us: local(): lax.psum_scatter(col_sums(hidden_picked, down_blocks, down_cols, d_cols)....]
    pallas_call x0 -> x1, Pallas kernels: none -> 112 us  [local(): pl.pallas_call(kernel_body, out_shape=(rows, rows, owned, owned, owned),...]
    dot_general x15 -> x0, matrix products: 91.6 us -> none  [the longest x3 23.2 us: block_terms(): jnp.einsum('tkd,tke->kde', picked_left, picked_right, preferred_element_t...]
    all_gather x2 -> x0, waiting for transfers between devices: 73.5 us -> none  [the longest x1 46.3 us: local(): gathered = lax.all_gather(tokens, 'tensor', axis=0, tiled=True)]
    scatter x3 -> x0, local copies, waits for them, and re-layouts: 62.1 us -> none  [owner_buffer(): jnp.zeros((slot_total,) + terms.shape[1:], jnp.float32).at[slots].set(terms)]
    convert_element_type x4 -> x0, other arithmetic: 20.6 us -> none  [the longest x1 6.85 us: local(): owner_buffer(down_terms, down_slot[0], slot_total).astype(jnp.bfloat16)]
    gather x6 -> x0, local copies, waits for them, and re-layouts: 17.3 us -> none  [the longest x1 2.9 us: local(): tokens_gate = jnp.take(token_blocks, gate_rows, axis=1)]
    another operation x3 -> x0, local copies, waits for them, and re-layouts: 13.7 us -> none
  transfers between devices with their start and end apart: 7 -> 0, of which waited for: 5 -> 0; matrix products, arithmetic and copies ran while one was open for 31% -> 0% of each run, Pallas kernels for 0% -> 0%
where the time goes in v1:
time: 126 us; the launch traced here: 125 us
  Pallas kernels  112 us (89%)
  local copies, waits for them, and re-layouts  8.7 us (7%)
  other arithmetic  3.27 us (3%)
    pallas_call x1, Pallas kernels, local(): pl.pallas_call(kernel_body, out_shape=(rows, rows, owned, owned, owned),...  112 us
    unnamed x9, local copies, waits for them, and re-layouts  8.02 us

profile of v1, /device:TPU:0, one launch (start us, length us, event | category | flops | bytes accessed | tf_op | source)
XLA Modules:
  0.0 125.0 jit_solution(14935679422676057617)
XLA Ops:
  0.7 0.7 fusion.14
  1.3 0.7 fusion.9
  2.0 1.0 fusion.8
  3.0 0.9 select_reduce_fusion
  3.9 0.7 concatenate.3.tab
  4.6 112.3 %shard_map.146 = (bf16[8,4096]{1,0:T(8,128)(2,1)}, bf16[8,4096]{1,0:T(8,128)(2,1)}, f32[17,128,128]{2,1,0:T(8,128)}, f32[17,128,128]{2,1,0:T(8,128)}, f32[17,128,128]{2,1,0:T(8,128)}) custom-call(s32[825]{0:T(1024)} %concatenate.3.tab, bf16[8,4096]{1,0:T(8,128)(2,1)} %tok_ref.1, bf16[8,4096]{1,0:T(8,128)(2,1)} %cot_ref.1, bf16[112,128,128]{2,1,0:T(8,128)(2,1)} %gb_ref.1, ...), custom_call_target="tpu_custom_call" | custom-call | tf_op jit(solution)/shard_map/pallas_call | solution.py:425
  117.0 1.5 %copy.21 = bf16[8,4096]{1,0:T(8,128)(2,1)} copy(bf16[8,4096]{1,0:T(8,128)(2,1)} %get-tuple-element.48) | data formatting | bytes 131072
  118.4 1.5 %copy.22 = bf16[8,4096]{1,0:T(8,128)(2,1)} copy(bf16[8,4096]{1,0:T(8,128)(2,1)} %get-tuple-element.49) | data formatting | bytes 131072
  119.9 0.0 copy-start.1
  119.9 2.4 %copy.23 = f32[1,17,128,128]{3,2,1,0:T(8,128)} copy(f32[1,17,128,128]{3,2,1,0:T(8,128)} %bitcast.23) | data formatting | bytes 2228224
  122.4 0.0 copy-done.1
  122.4 0.0 copy-start
  122.4 1.0 copy.24
  123.4 0.7 copy-done
  124.0 1.0 copy.25
  (4 shorter events, 0.0 us)
Async XLA Ops:
  119.9 2.4 %copy-start.1 = (f32[17,128,128]{2,1,0:T(8,128)S(1)}, f32[17,128,128]{2,1,0:T(8,128)}, u32[]{:S(2)}) copy-start(f32[17,128,128]{2,1,0:T(8,128)} %get-tuple-element.13) | copy-start | bytes 3342340
  122.4 1.6 %copy-start = (f32[17,128,128]{2,1,0:T(8,128)S(1)}, f32[17,128,128]{2,1,0:T(8,128)}, u32[]{:S(2)}) copy-start(f32[17,128,128]{2,1,0:T(8,128)} %get-tuple-element.14) | copy-start | bytes 3342340

commit v2 on v1

v2 whole, which is shorter than its diff:
```python
import functools
import math

import jax
import jax.numpy as jnp
from jax import lax
from jax.experimental import pallas as pl
from jax.experimental.pallas import tpu as pltpu
from jax.sharding import PartitionSpec as P

MESH = pl.DeviceIdType.MESH
D = 4096
BLK = 128
DC = 32
FC = 7
FDEV = 896
KB = 112
NBLK = 224
CAP = 17
TOK = 1024
F32 = jnp.float32
BF16 = jnp.bfloat16

THIRDS = ((0, 6, 12), (12, 17, 22), (22, 27, 32))
ORDERS = (("x", "y", "z"), ("y", "z", "x"), ("z", "x", "y"))


def kernel_body(
    tok_ref,
    cot_ref,
    gb_ref,
    ub_ref,
    db_ref,
    gi_ref,
    ui_ref,
    di_ref,
    gs_ref,
    us_ref,
    ds_ref,
    lo_ref,
    tg_ref,
    gg_ref,
    ug_ref,
    dg_ref,
    gi,
    ui,
    di,
    giv,
    uiv,
    div,
    gsv,
    usv,
    dsv,
    picks,
    taken,
    where,
    buf,
    wgu,
    wd,
    stage,
    acc,
    hid,
    gpre,
    part,
    got1,
    got2,
    mid,
    got3,
    rows_out,
    grad_out,
    in_sem,
    ld_sem,
    out_sem,
    ag_send,
    ag_recv,
    sib_send,
    sib_recv,
    rs_send,
    rs_recv,
):
    dp = lax.axis_index("dp")
    tp = lax.axis_index("tensor")
    ylo, z = dp // 4, dp % 4
    x, yhi, core = tp // 4, (tp // 2) % 2, tp % 2
    y = yhi * 2 + ylo
    here = {"x": x, "y": y, "z": z}

    def device(at, c):
        return (
            (at["y"] % 2) * 4 + at["z"],
            at["x"] * 4 + (at["y"] // 2) * 2 + c,
        )

    def moved(axis, step):
        at = dict(here)
        at[axis] = (here[axis] + step) % 4
        return at

    right = {a: device(moved(a, 1), core) for a in "xyz"}
    left = {a: device(moved(a, 3), core) for a in "xyz"}
    far = {a: device(moved(a, 2), core) for a in "xyz"}
    sibling = device(here, 1 - core)

    small = [
        pltpu.make_async_copy(src, dst, in_sem.at[n])
        for n, (src, dst) in enumerate(
            (
                (gi_ref, gi),
                (ui_ref, ui),
                (di_ref, di),
                (gi_ref, giv),
                (ui_ref, uiv),
                (di_ref, div),
                (gs_ref, gsv),
                (us_ref, usv),
                (ds_ref, dsv),
            )
        )
    ]

    def load(src):
        return pltpu.make_async_copy(src, stage.at[pl.ds(0, KB)], ld_sem)

    barrier = pltpu.get_barrier_semaphore()
    partners = list(right.values()) + list(left.values()) + list(far.values()) + [sibling]
    for other in partners:
        pl.semaphore_signal(barrier, inc=1, device_id=other, device_id_type=MESH)
    for copy in small:
        copy.start()
    load(gb_ref).start()
    for j in range(DC):
        cols = pl.ds(j * BLK, BLK)
        buf[0, j, z, y, x, core] = tok_ref[:, cols]
        buf[1, j, z, y, x, core] = cot_ref[:, cols]
    pl.semaphore_wait(barrier, len(partners))

    def plane(axis, along):
        return tuple(along if a == axis else slice(None) for a in ("z", "y", "x"))

    def region(q, third, phase, along, lo, hi):
        axes = ORDERS[third]
        idx = []
        for a in ("z", "y", "x"):
            if a in axes[:phase]:
                idx.append(slice(None))
            elif a == axes[phase]:
                idx.append(along)
            else:
                idx.append(here[a])
        return buf.at[(q, pl.ds(lo, hi - lo), *idx, core)]

    def ag_copy(q, third, phase, k):
        lo, mid_col, hi = THIRDS[third]
        axis = ORDERS[third][phase]
        own = here[axis]
        if phase == 0:
            along, cols, to = own, (lo, hi), (right, left, far)[k]
        else:
            along, cols, to = (
                (own, (lo, mid_col), right),
                (own, (mid_col, hi), left),
                (own, (mid_col, hi), right),
                (own, (lo, mid_col), left),
                ((own + 3) % 4, (lo, mid_col), right),
                ((own + 1) % 4, (mid_col, hi), left),
            )[k]
        ref = region(q, third, phase, along, *cols)
        return pltpu.make_async_remote_copy(
            src_ref=ref,
            dst_ref=ref,
            send_sem=ag_send.at[q, third, phase, k],
            recv_sem=ag_recv.at[q, third, phase, k],
            device_id=to[axis],
            device_id_type=MESH,
        )

    def sib_copy(q, third, k):
        lo, _, hi = THIRDS[third]
        axis = ORDERS[third][2]
        ref = region(q, third, 2, (here[axis] + k) % 4, lo, hi)
        return pltpu.make_async_remote_copy(
            src_ref=ref,
            dst_ref=ref,
            send_sem=sib_send.at[q, third, k],
            recv_sem=sib_recv.at[q, third, k],
            device_id=sibling,
            device_id_type=MESH,
        )

    def ag_start(q, phase):
        for k in range(4 if phase else 3):
            for third in range(3):
                ag_copy(q, third, phase, k).start()

    def ag_line(q):
        for third in range(3):
            for k in range(3):
                ag_copy(q, third, 0, k).wait_recv()

    def ag_forward(q, phase):
        for third in range(3):
            ag_copy(q, third, phase, 0).wait_recv()
            ag_copy(q, third, phase, 4).start()
            ag_copy(q, third, phase, 1).wait_recv()
            ag_copy(q, third, phase, 5).start()

    def ag_direct(q, phase):
        for third in range(3):
            ag_copy(q, third, phase, 2).wait_recv()
            ag_copy(q, third, phase, 3).wait_recv()

    def ag_far(q, phase):
        for third in range(3):
            ag_copy(q, third, phase, 4).wait_recv()
            ag_copy(q, third, phase, 5).wait_recv()

    def sib_start(q, k):
        for third in range(3):
            sib_copy(q, third, k).start()

    def sib_wait(q, third, k):
        sib_copy(q, third, k).wait_recv()

    def ag_finish(q):
        for third in range(3):
            for k in range(3):
                ag_copy(q, third, 0, k).wait_send()
            for phase in (1, 2):
                for k in range(6):
                    ag_copy(q, third, phase, k).wait_send()
            for k in range(4):
                sib_copy(q, third, k).wait_send()

    def find_blocks():
        for n in range(3):
            taken[n] = 0

        @pl.loop(0, DC)
        def _(r):
            for c in range(FC):
                number = r * FC + c
                for n, ids in enumerate((gi, ui, di)):
                    at = jnp.minimum(taken[n], KB - 1)
                    hit = ids[0, at] == number
                    where[n, number] = jnp.where(hit, at, KB)
                    taken[n] = taken[n] + hit.astype(jnp.int32)

    def spread(n, per, store, lo, hi):
        @pl.loop(lo, hi)
        def _(r):
            for c in range(per):
                store(r, c, stage[where[n, r * per + c]])

    def block_rows(r):
        return pl.ds(pl.multiple_of(r * BLK, BLK), BLK)

    def store_gate(r, c, block):
        wgu[c, block_rows(r), pl.ds(0, BLK)] = block

    def store_up(r, c, block):
        wgu[c, block_rows(r), pl.ds(BLK, BLK)] = block

    def store_down(r, c, block):
        wd[block_rows(r), pl.ds(c * BLK, BLK)] = block

    def rows_at(q, third, ks):
        lo, _, hi = THIRDS[third]
        axis = ORDERS[third][2]
        runs = []
        for k in ks:
            at = plane(axis, (here[axis] + k) % 4)
            runs.append(
                jnp.concatenate(
                    [buf[(q, j, *at)].reshape(256, BLK) for j in range(lo, hi)], axis=1
                )
            )
        return jnp.concatenate(runs, axis=0)

    def add_to(n, third, ks, term):
        axis = ORDERS[third][2]
        for s, k in enumerate(ks):
            at = (n, *plane(axis, (here[axis] + k) % 4))
            acc[at] = acc[at] + term[s * 256 : (s + 1) * 256].reshape(4, 4, 16, BLK)

    def forward_step(third, ks):
        lo, _, hi = THIRDS[third]
        for k in ks:
            sib_wait(0, third, k)

        @pl.loop(0, FC)
        def _(c):
            both = jnp.dot(
                rows_at(0, third, ks),
                wgu[c, pl.ds(lo * BLK, (hi - lo) * BLK), :],
                preferred_element_type=F32,
            )
            add_to(2 * c, third, ks, both[:, :BLK])
            add_to(2 * c + 1, third, ks, both[:, BLK:])

    def backward_step(third, ks):
        lo, _, hi = THIRDS[third]
        for k in ks:
            sib_wait(1, third, k)

        def some(start, width):
            grad = lax.dot_general(
                rows_at(1, third, ks),
                wd[pl.ds(start * BLK, width * BLK), pl.ds(lo * BLK, (hi - lo) * BLK)],
                (((1,), (1,)), ((), ())),
                preferred_element_type=F32,
            )
            for j in range(width):
                add_to(start + j, third, ks, grad[:, j * BLK : (j + 1) * BLK])

        @pl.loop(0, 3)
        def _(c):
            some(2 * c, 2)

        some(6, 1)

    def point_forward():
        @pl.loop(0, FC)
        def _(c):
            @pl.loop(0, 4)
            def _(m):
                rows = pl.ds(pl.multiple_of(m * 256, 256), 256)
                gate = acc[2 * c, m].reshape(256, BLK)
                up = acc[2 * c + 1, m].reshape(256, BLK)
                sigma = 1.0 / (1.0 + jnp.exp(-gate))
                swish = gate * sigma
                hid[c, rows, :] = (swish * up).astype(BF16)
                gpre[2 * c, rows, :] = (up * sigma * (1.0 + gate * (1.0 - sigma))).astype(BF16)
                gpre[2 * c + 1, rows, :] = swish.astype(BF16)
                acc[2 * c, m] = jnp.zeros((4, 4, 16, BLK), F32)
                acc[2 * c + 1, m] = jnp.zeros((4, 4, 16, BLK), F32)

    def point_backward():
        @pl.loop(0, FC)
        def _(c):
            @pl.loop(0, 4)
            def _(m):
                rows = pl.ds(pl.multiple_of(m * 256, 256), 256)
                grad = acc[c, m].reshape(256, BLK)
                for side in range(2):
                    gpre[2 * c + side, rows, :] = (
                        gpre[2 * c + side, rows, :].astype(F32) * grad
                    ).astype(BF16)

    def own_rows(ref):
        runs = []
        for h in range(2):
            rows = pl.ds(pl.multiple_of((z * 4 + h * 2 + ylo) * 64, 64), 64)
            runs.append(jnp.concatenate([ref[j, rows, :] for j in range(ref.shape[0])], axis=1))
        return jnp.concatenate(runs, axis=0)

    def partial_out(o):
        width = 512

        @pl.loop(0, D // width)
        def _(n):
            cols = pl.ds(pl.multiple_of(n * width, width), width)
            if o == 0:
                term = jnp.dot(own_rows(hid), wd[:, cols], preferred_element_type=F32)
            else:
                term = lax.dot_general(
                    own_rows(gpre),
                    jnp.concatenate([wgu[c, cols, :] for c in range(FC)], axis=1),
                    (((1,), (1,)), ((), ())),
                    preferred_element_type=F32,
                )
            part[o, :, :, :, :, cols] = term.astype(BF16).reshape(2, 4, 2, 8, width)

    def rs_copy(o, k):
        if k == 0:
            src, dst, to = part.at[o, :, :, 1 - core], got1.at[o], sibling
        elif k < 4:
            at = moved("x", k)
            src, dst, to = part.at[o, :, at["x"], core], got2.at[o, k - 1], device(at, core)
        else:
            src, dst, to = mid.at[o, 1 - yhi], got3.at[o], far["y"]
        return pltpu.make_async_remote_copy(
            src_ref=src,
            dst_ref=dst,
            send_sem=rs_send.at[o, k],
            recv_sem=rs_recv.at[o, k],
            device_id=to,
            device_id_type=MESH,
        )

    def rs_one(o):
        rs_copy(o, 0).start()

    def rs_two(o):
        rs_copy(o, 0).wait_recv()
        for h in range(2):
            for w in range(4):
                part[o, h, w, core] = (
                    part[o, h, w, core].astype(F32) + got1[o, h, w].astype(F32)
                ).astype(BF16)
        for k in (2, 1, 3):
            rs_copy(o, k).start()

    def rs_three(o):
        for k in range(1, 4):
            rs_copy(o, k).wait_recv()
        for h in range(2):
            total = part[o, h, x, core].astype(F32)
            for k in range(3):
                total = total + got2[o, k, h].astype(F32)
            mid[o, h] = total.astype(BF16)
        rs_copy(o, 4).start()

    def row_copy(o):
        return pltpu.make_async_copy(rows_out.at[o], (lo_ref, tg_ref)[o], out_sem.at[o])

    def rs_four(o):
        rs_copy(o, 4).wait_recv()
        rows_out[o] = (mid[o, yhi].astype(F32) + got3[o].astype(F32)).astype(BF16)
        row_copy(o).start()
        for k in range(5):
            rs_copy(o, k).wait_send()

    def pick_slots():
        @pl.loop(0, CAP)
        def _(v):
            mine = dp * CAP + v
            for n, (ids, slots) in enumerate(((giv, gsv), (uiv, usv), (div, dsv))):
                picks[n, v] = jnp.sum(jnp.where(slots[...] == mine, ids[...] + 1, 0))

    factor = 1.0 / math.sqrt(TOK)

    def block_grad(left, right, weight):
        return (
            lax.dot_general(left, right, (((0,), (0,)), ((), ())), preferred_element_type=F32)
            * weight
        )

    def grads(lo, hi):
        @pl.loop(lo, hi)
        def _(v):
            for n in range(3):
                number = picks[n, v]
                block = jnp.maximum(number - 1, 0)
                weight = jnp.where(number > 0, factor, 0.0)
                if n < 2:
                    left = buf[0, block // FC].reshape(TOK, BLK)
                    right = gpre[2 * (block % FC) + n]
                else:
                    left = hid[block // DC]
                    right = buf[1, block % DC].reshape(TOK, BLK)
                grad_out[n, v] = block_grad(left, right, weight)

    def grad_copy(n):
        return pltpu.make_async_copy(grad_out.at[n], (gg_ref, ug_ref, dg_ref)[n], out_sem.at[2 + n])

    ag_start(0, 0)
    ag_start(1, 0)
    stage[KB] = jnp.zeros((BLK, BLK), BF16)
    for copy in small:
        copy.wait()

    @pl.loop(0, 2 * FC)
    def _(n):
        acc[n] = jnp.zeros((4, 4, 4, 16, BLK), F32)

    find_blocks()
    ag_line(0)
    ag_start(0, 1)
    load(gb_ref).wait()
    spread(0, FC, store_gate, 0, 8)
    ag_line(1)
    ag_start(1, 1)
    spread(0, FC, store_gate, 8, 16)
    ag_forward(0, 1)
    spread(0, FC, store_gate, 16, DC)
    load(ub_ref).start()
    ag_direct(0, 1)
    ag_far(0, 1)
    ag_start(0, 2)
    sib_start(0, 0)
    ag_forward(1, 1)
    load(ub_ref).wait()
    spread(1, FC, store_up, 0, 16)
    ag_direct(1, 1)
    ag_far(1, 1)
    sib_start(1, 0)
    spread(1, FC, store_up, 16, DC)
    load(db_ref).start()
    forward_step(0, (0,))
    ag_forward(0, 2)
    forward_step(1, (0,))
    forward_step(2, (0,))
    load(db_ref).wait()
    spread(2, DC, store_down, 0, FC)
    ag_direct(0, 2)
    ag_start(1, 2)
    sib_start(0, 1)
    sib_start(0, 3)
    pick_slots()
    forward_step(0, (1, 3))
    ag_far(0, 2)
    sib_start(0, 2)
    forward_step(1, (1, 3))
    ag_forward(1, 2)
    forward_step(2, (1, 3))
    for third in range(3):
        forward_step(third, (2,))
    point_forward()
    ag_direct(1, 2)
    sib_start(1, 1)
    sib_start(1, 3)
    partial_out(0)
    rs_one(0)
    for third in range(3):
        backward_step(third, (0,))
    rs_two(0)
    ag_far(1, 2)
    sib_start(1, 2)
    for third in range(3):
        backward_step(third, (1, 3))
    rs_three(0)
    for third in range(3):
        backward_step(third, (2,))
    point_backward()
    partial_out(1)
    rs_one(1)
    grads(0, 3)
    rs_two(1)
    rs_four(0)
    grads(3, 9)
    rs_three(1)
    grads(9, 13)
    rs_four(1)
    grads(13, CAP)
    for n in range(3):
        grad_copy(n).start()
    ag_finish(0)
    ag_finish(1)
    for o in range(2):
        row_copy(o).wait()
    for n in range(3):
        grad_copy(n).wait()


def copy_body(*refs):
    sources, targets, sem = refs[:5], refs[5:10], refs[10]
    copies = [pltpu.make_async_copy(a, b, sem.at[n]) for n, (a, b) in enumerate(zip(sources, targets))]
    for copy in copies:
        copy.start()
    for copy in copies:
        copy.wait()


def local(
    tokens,
    out_grad,
    gate_blocks,
    up_blocks,
    down_blocks,
    gate_index,
    up_index,
    down_index,
    gate_slot,
    up_slot,
    down_slot,
):
    hbm = pl.BlockSpec(memory_space=pl.ANY)
    vmem = pl.BlockSpec(memory_space=pltpu.VMEM)
    rows = jax.ShapeDtypeStruct((8, D), BF16)
    owned = jax.ShapeDtypeStruct((CAP, BLK, BLK), F32)
    shapes = (rows, rows, owned, owned, owned)
    results = pl.pallas_call(
        kernel_body,
        out_shape=shapes,
        in_specs=[vmem, vmem] + [hbm] * 9,
        out_specs=(hbm,) * 5,
        scratch_shapes=[pltpu.SMEM((1, KB), jnp.int32)] * 3
        + [pltpu.VMEM((1, KB), jnp.int32)] * 6
        + [
            pltpu.SMEM((3, CAP), jnp.int32),
            pltpu.SMEM((3,), jnp.int32),
            pltpu.SMEM((3, NBLK), jnp.int32),
            pltpu.VMEM((2, DC, 4, 4, 4, 2, 8, BLK), BF16),
            pltpu.VMEM((FC, D, 2 * BLK), BF16),
            pltpu.VMEM((FDEV, D), BF16),
            pltpu.VMEM((KB + 1, BLK, BLK), BF16),
            pltpu.VMEM((2 * FC, 4, 4, 4, 16, BLK), F32),
            pltpu.VMEM((FC, TOK, BLK), BF16),
            pltpu.VMEM((2 * FC, TOK, BLK), BF16),
            pltpu.VMEM((2, 2, 4, 2, 8, D), BF16),
            pltpu.VMEM((2, 2, 4, 8, D), BF16),
            pltpu.VMEM((2, 3, 2, 8, D), BF16),
            pltpu.VMEM((2, 2, 8, D), BF16),
            pltpu.VMEM((2, 8, D), BF16),
            pltpu.VMEM((2, 8, D), BF16),
            pltpu.VMEM((3, CAP, BLK, BLK), F32),
            pltpu.SemaphoreType.DMA((9,)),
            pltpu.SemaphoreType.DMA,
            pltpu.SemaphoreType.DMA((5,)),
            pltpu.SemaphoreType.DMA((2, 3, 3, 6)),
            pltpu.SemaphoreType.DMA((2, 3, 3, 6)),
            pltpu.SemaphoreType.DMA((2, 3, 4)),
            pltpu.SemaphoreType.DMA((2, 3, 4)),
            pltpu.SemaphoreType.DMA((2, 5)),
            pltpu.SemaphoreType.DMA((2, 5)),
        ],
        compiler_params=pltpu.CompilerParams(
            collective_id=0, has_side_effects=True, vmem_limit_bytes=62 * 1024 * 1024
        ),
    )(
        tokens,
        out_grad,
        gate_blocks,
        up_blocks,
        down_blocks,
        gate_index,
        up_index,
        down_index,
        gate_slot,
        up_slot,
        down_slot,
    )
    lo, tg, gg, ug, dg = pl.pallas_call(
        copy_body,
        out_shape=shapes,
        in_specs=[hbm] * 5,
        out_specs=(hbm,) * 5,
        scratch_shapes=[pltpu.SemaphoreType.DMA((5,))],
    )(*results)
    return lo, tg, gg[None], ug[None], dg[None]


def solution(mesh):
    in_specs = (
        P(("dp", "tensor"), None),
        P(("dp", "tensor"), None),
        P("tensor", None, None),
        P("tensor", None, None),
        P("tensor", None, None),
        P("tensor", None),
        P("tensor", None),
        P("tensor", None),
        P("tensor", None),
        P("tensor", None),
        P("tensor", None),
    )
    out_specs = (
        P(("dp", "tensor"), None),
        P(("dp", "tensor"), None),
        P("tensor", "dp", None, None),
        P("tensor", "dp", None, None),
        P("tensor", "dp", None, None),
    )
    return jax.shard_map(local, mesh=mesh, in_specs=in_specs, out_specs=out_specs, check_vma=False)
```

time: 126 us -> 217 us (1.72)
  Pallas kernels: 112 us -> 216 us
  local copies, waits for them, and re-layouts: 8.7 us -> 0 us
  other arithmetic: 3.27 us -> 0 us
    pallas_call x1 -> x2, Pallas kernels: 112 us -> 216 us  [the longest x1 110 us: local(): pl.pallas_call(kernel_body, out_shape=shapes, in_specs=[vmem, vmem] + [hb...]
    unnamed x9 -> x0, local copies, waits for them, and re-layouts: 8.02 us -> none
where the time goes in v2:
time: 217 us
  Pallas kernels  216 us (100%)
    pallas_call x1, Pallas kernels, local(): pl.pallas_call(kernel_body, out_shape=shapes, in_specs=[vmem, vmem] + [hb...  110 us
    pallas_call x1, Pallas kernels, local(): pl.pallas_call(copy_body, out_shape=shapes, in_specs=[hbm] * 5, out_specs...  106 us

profile of v2, /device:TPU:0, one launch (start us, length us, event | category | flops | bytes accessed | tf_op | source)
XLA Modules:
  0.0 216.8 jit_solution(5675096494933246370)
XLA Ops:
  0.6 109.7 %shard_map.146 = (bf16[8,4096]{1,0:T(8,128)(2,1)}, bf16[8,4096]{1,0:T(8,128)(2,1)}, f32[17,128,128]{2,1,0:T(8,128)}, f32[17,128,128]{2,1,0:T(8,128)}, f32[17,128,128]{2,1,0:T(8,128)}) custom-call(bf16[8,4096]{1,0:T(8,128)(2,1)} %tok_ref.1, bf16[8,4096]{1,0:T(8,128)(2,1)} %cot_ref.1, bf16[112,128,128]{2,1,0:T(8,128)(2,1)} %gb_ref.1, ...), custom_call_target="tpu_custom_call" | custom-call | tf_op jit(solution)/shard_map/pallas_call | solution.py:572
  110.4 106.4 %shard_map.147 = (bf16[8,4096]{1,0:T(8,128)(2,1)}, bf16[8,4096]{1,0:T(8,128)(2,1)}, f32[17,128,128]{2,1,0:T(8,128)}, f32[17,128,128]{2,1,0:T(8,128)}, f32[17,128,128]{2,1,0:T(8,128)}) custom-call(bf16[8,4096]{1,0:T(8,128)(2,1)} %get-tuple-element.15.refs_0_, bf16[8,4096]{1,0:T(8,128)(2,1)} %get-tuple-element.16.refs_1_, ...), custom_call_target="tpu_custom_call" | custom-call | tf_op jit(solution)/shard_map/pallas_call | solution.py:623

commit v3 on v2

--- a/solution.py
+++ b/solution.py
@@ -58,9 +58,9 @@
     wgu,
     wd,
     stage,
-    acc,
     hid,
     gpre,
+    own_g,
     part,
     got1,
     got2,
@@ -130,12 +130,9 @@
     load(gb_ref).start()
     for j in range(DC):
         cols = pl.ds(j * BLK, BLK)
-        buf[0, j, z, y, x, core] = tok_ref[:, cols]
-        buf[1, j, z, y, x, core] = cot_ref[:, cols]
+        buf[0, j, core, z, y, x] = tok_ref[:, cols]
+        buf[1, j, core, z, y, x] = cot_ref[:, cols]
     pl.semaphore_wait(barrier, len(partners))
-
-    def plane(axis, along):
-        return tuple(along if a == axis else slice(None) for a in ("z", "y", "x"))
 
     def region(q, third, phase, along, lo, hi):
         axes = ORDERS[third]
@@ -147,13 +144,13 @@
                 idx.append(along)
             else:
                 idx.append(here[a])
-        return buf.at[(q, pl.ds(lo, hi - lo), *idx, core)]
+        return buf.at[(q, pl.ds(lo, hi - lo), core, *idx)]
 
     def ag_copy(q, third, phase, k):
         lo, mid_col, hi = THIRDS[third]
         axis = ORDERS[third][phase]
         own = here[axis]
-        if phase == 0:
+        if phase < 2:
             along, cols, to = own, (lo, hi), (right, left, far)[k]
         else:
             along, cols, to = (
@@ -188,45 +185,45 @@
         )
 
     def ag_start(q, phase):
-        for k in range(4 if phase else 3):
+        for k in range(4 if phase == 2 else 3):
             for third in range(3):
                 ag_copy(q, third, phase, k).start()
 
-    def ag_line(q):
+    def ag_wait(q, phase):
         for third in range(3):
             for k in range(3):
-                ag_copy(q, third, 0, k).wait_recv()
-
-    def ag_forward(q, phase):
+                ag_copy(q, third, phase, k).wait_recv()
+
+    def ag_forward(q):
         for third in range(3):
-            ag_copy(q, third, phase, 0).wait_recv()
-            ag_copy(q, third, phase, 4).start()
-            ag_copy(q, third, phase, 1).wait_recv()
-            ag_copy(q, third, phase, 5).start()
-
-    def ag_direct(q, phase):
+            ag_copy(q, third, 2, 0).wait_recv()
+            ag_copy(q, third, 2, 4).start()
+            ag_copy(q, third, 2, 1).wait_recv()
+            ag_copy(q, third, 2, 5).start()
+
+    def ag_direct(q):
         for third in range(3):
-            ag_copy(q, third, phase, 2).wait_recv()
-            ag_copy(q, third, phase, 3).wait_recv()
-
-    def ag_far(q, phase):
+            ag_copy(q, third, 2, 2).wait_recv()
+            ag_copy(q, third, 2, 3).wait_recv()
+
+    def ag_far(q):
         for third in range(3):
-            ag_copy(q, third, phase, 4).wait_recv()
-            ag_copy(q, third, phase, 5).wait_recv()
+            ag_copy(q, third, 2, 4).wait_recv()
+            ag_copy(q, third, 2, 5).wait_recv()
 
     def sib_start(q, k):
         for third in range(3):
             sib_copy(q, third, k).start()
 
-    def sib_wait(q, third, k):
-        sib_copy(q, third, k).wait_recv()
+    def sib_wait(q):
+        for third in range(3):
+            for k in range(4):
+                sib_copy(q, third, k).wait_recv()
 
     def ag_finish(q):
         for third in range(3):
-            for k in range(3):
-                ag_copy(q, third, 0, k).wait_send()
-            for phase in (1, 2):
-                for k in range(6):
+            for phase in range(3):
+                for k in range(6 if phase == 2 else 3):
                     ag_copy(q, third, phase, k).wait_send()
             for k in range(4):
                 sib_copy(q, third, k).wait_send()
@@ -263,95 +260,63 @@
     def store_down(r, c, block):
         wd[block_rows(r), pl.ds(c * BLK, BLK)] = block
 
-    def rows_at(q, third, ks):
-        lo, _, hi = THIRDS[third]
-        axis = ORDERS[third][2]
-        runs = []
-        for k in ks:
-            at = plane(axis, (here[axis] + k) % 4)
-            runs.append(
-                jnp.concatenate(
-                    [buf[(q, j, *at)].reshape(256, BLK) for j in range(lo, hi)], axis=1
-                )
-            )
-        return jnp.concatenate(runs, axis=0)
-
-    def add_to(n, third, ks, term):
-        axis = ORDERS[third][2]
-        for s, k in enumerate(ks):
-            at = (n, *plane(axis, (here[axis] + k) % 4))
-            acc[at] = acc[at] + term[s * 256 : (s + 1) * 256].reshape(4, 4, 16, BLK)
-
-    def forward_step(third, ks):
-        lo, _, hi = THIRDS[third]
-        for k in ks:
-            sib_wait(0, third, k)
-
-        @pl.loop(0, FC)
+    flat = buf.reshape(2, DC, TOK, BLK)
+
+    def rows_of(q, rows):
+        return jnp.concatenate([flat[q, j, rows, :] for j in range(DC)], axis=1)
+
+    def forward_cols(lo, hi, start, size):
+        @pl.loop(lo, hi)
         def _(c):
-            both = jnp.dot(
-                rows_at(0, third, ks),
-                wgu[c, pl.ds(lo * BLK, (hi - lo) * BLK), :],
-                preferred_element_type=F32,
-            )
-            add_to(2 * c, third, ks, both[:, :BLK])
-            add_to(2 * c + 1, third, ks, both[:, BLK:])
-
-    def backward_step(third, ks):
-        lo, _, hi = THIRDS[third]
-        for k in ks:
-            sib_wait(1, third, k)
-
-        def some(start, width):
-            grad = lax.dot_general(
-                rows_at(1, third, ks),
-                wd[pl.ds(start * BLK, width * BLK), pl.ds(lo * BLK, (hi - lo) * BLK)],
-                (((1,), (1,)), ((), ())),
-                preferred_element_type=F32,
-            )
-            for j in range(width):
-                add_to(start + j, third, ks, grad[:, j * BLK : (j + 1) * BLK])
-
-        @pl.loop(0, 3)
-        def _(c):
-            some(2 * c, 2)
-
-        some(6, 1)
-
-    def point_forward():
-        @pl.loop(0, FC)
-        def _(c):
-            @pl.loop(0, 4)
-            def _(m):
-                rows = pl.ds(pl.multiple_of(m * 256, 256), 256)
-                gate = acc[2 * c, m].reshape(256, BLK)
-                up = acc[2 * c + 1, m].reshape(256, BLK)
+            for rows in [pl.ds(start, size)]:
+                both = jnp.dot(rows_of(0, rows), wgu[c], preferred_element_type=F32)
+                gate, up = both[:, :BLK], both[:, BLK:]
                 sigma = 1.0 / (1.0 + jnp.exp(-gate))
                 swish = gate * sigma
                 hid[c, rows, :] = (swish * up).astype(BF16)
                 gpre[2 * c, rows, :] = (up * sigma * (1.0 + gate * (1.0 - sigma))).astype(BF16)
                 gpre[2 * c + 1, rows, :] = swish.astype(BF16)
-                acc[2 * c, m] = jnp.zeros((4, 4, 16, BLK), F32)
-                acc[2 * c + 1, m] = jnp.zeros((4, 4, 16, BLK), F32)
-
-    def point_backward():
-        @pl.loop(0, FC)
-        def _(c):
-            @pl.loop(0, 4)
-            def _(m):
-                rows = pl.ds(pl.multiple_of(m * 256, 256), 256)
-                grad = acc[c, m].reshape(256, BLK)
+
+    def backward_cols(start, width):
+        for rows in [pl.ds(0, TOK)]:
+            w = wd[pl.ds(pl.multiple_of(start * BLK, BLK), width * BLK), :]
+            grad = lax.dot_general(
+                rows_of(1, rows), w, (((1,), (1,)), ((), ())), preferred_element_type=F32
+            )
+            for j in range(width):
+                piece = grad[:, j * BLK : (j + 1) * BLK]
                 for side in range(2):
-                    gpre[2 * c + side, rows, :] = (
-                        gpre[2 * c + side, rows, :].astype(F32) * grad
-                    ).astype(BF16)
-
-    def own_rows(ref):
+                    k = 2 * (start + j) + side
+                    gpre[k, rows, :] = (gpre[k, rows, :].astype(F32) * piece).astype(BF16)
+
+    def own_rows(ref, *lead):
         runs = []
         for h in range(2):
-            rows = pl.ds(pl.multiple_of((z * 4 + h * 2 + ylo) * 64, 64), 64)
-            runs.append(jnp.concatenate([ref[j, rows, :] for j in range(ref.shape[0])], axis=1))
+            for c in range(2):
+                at = c * 512 + (z * 4 + h * 2 + ylo) * 32
+                rows = pl.ds(pl.multiple_of(at, 32), 32)
+                blocks = ref.shape[len(lead)]
+                runs.append(
+                    jnp.concatenate([ref[(*lead, j, rows)] for j in range(blocks)], axis=1)
+                )
         return jnp.concatenate(runs, axis=0)
+
+    def own_backward(start, width):
+        w = wd[pl.ds(pl.multiple_of(start * BLK, BLK), width * BLK), :]
+        grad = lax.dot_general(
+            own_rows(flat, 1), w, (((1,), (1,)), ((), ())), preferred_element_type=F32
+        )
+        for j in range(width):
+            piece = grad[:, j * BLK : (j + 1) * BLK]
+            for side in range(2):
+                k = 2 * (start + j) + side
+                runs = []
+                for h in range(2):
+                    for c in range(2):
+                        at = c * 512 + (z * 4 + h * 2 + ylo) * 32
+                        runs.append(gpre[k, pl.ds(pl.multiple_of(at, 32), 32), :])
+                slope = jnp.concatenate(runs, axis=0).astype(F32)
+                own_g[k] = (slope * piece).astype(BF16)
 
     def partial_out(o):
         width = 512
@@ -363,19 +328,19 @@
                 term = jnp.dot(own_rows(hid), wd[:, cols], preferred_element_type=F32)
             else:
                 term = lax.dot_general(
-                    own_rows(gpre),
+                    jnp.concatenate([own_g[k] for k in range(2 * FC)], axis=1),
                     jnp.concatenate([wgu[c, cols, :] for c in range(FC)], axis=1),
                     (((1,), (1,)), ((), ())),
                     preferred_element_type=F32,
                 )
-            part[o, :, :, :, :, cols] = term.astype(BF16).reshape(2, 4, 2, 8, width)
+            part[o, :, :, :, :, cols] = term.astype(BF16).reshape(2, 2, 4, 8, width)
 
     def rs_copy(o, k):
         if k == 0:
-            src, dst, to = part.at[o, :, :, 1 - core], got1.at[o], sibling
+            src, dst, to = part.at[o, :, 1 - core], got1.at[o], sibling
         elif k < 4:
             at = moved("x", k)
-            src, dst, to = part.at[o, :, at["x"], core], got2.at[o, k - 1], device(at, core)
+            src, dst, to = part.at[o, :, core, at["x"]], got2.at[o, k - 1], device(at, core)
         else:
             src, dst, to = mid.at[o, 1 - yhi], got3.at[o], far["y"]
         return pltpu.make_async_remote_copy(
@@ -394,8 +359,8 @@
         rs_copy(o, 0).wait_recv()
         for h in range(2):
             for w in range(4):
-                part[o, h, w, core] = (
-                    part[o, h, w, core].astype(F32) + got1[o, h, w].astype(F32)
+                part[o, h, core, w] = (
+                    part[o, h, core, w].astype(F32) + got1[o, h, w].astype(F32)
                 ).astype(BF16)
         for k in (2, 1, 3):
             rs_copy(o, k).start()
@@ -404,7 +369,7 @@
         for k in range(1, 4):
             rs_copy(o, k).wait_recv()
         for h in range(2):
-            total = part[o, h, x, core].astype(F32)
+            total = part[o, h, core, x].astype(F32)
             for k in range(3):
                 total = total + got2[o, k, h].astype(F32)
             mid[o, h] = total.astype(BF16)
@@ -453,85 +418,79 @@
     def grad_copy(n):
         return pltpu.make_async_copy(grad_out.at[n], (gg_ref, ug_ref, dg_ref)[n], out_sem.at[2 + n])
 
+    mine, other = core * 512, (1 - core) * 512
     ag_start(0, 0)
-    ag_start(1, 0)
     stage[KB] = jnp.zeros((BLK, BLK), BF16)
     for copy in small:
         copy.wait()
-
-    @pl.loop(0, 2 * FC)
-    def _(n):
-        acc[n] = jnp.zeros((4, 4, 4, 16, BLK), F32)
-
     find_blocks()
-    ag_line(0)
+    ag_wait(0, 0)
     ag_start(0, 1)
+    ag_start(1, 0)
     load(gb_ref).wait()
-    spread(0, FC, store_gate, 0, 8)
-    ag_line(1)
+    spread(0, FC, store_gate, 0, DC)
+    load(ub_ref).start()
+    ag_wait(0, 1)
+    ag_start(0, 2)
+    ag_wait(1, 0)
     ag_start(1, 1)
-    spread(0, FC, store_gate, 8, 16)
-    ag_forward(0, 1)
-    spread(0, FC, store_gate, 16, DC)
-    load(ub_ref).start()
-    ag_direct(0, 1)
-    ag_far(0, 1)
-    ag_start(0, 2)
     sib_start(0, 0)
-    ag_forward(1, 1)
     load(ub_ref).wait()
-    spread(1, FC, store_up, 0, 16)
-    ag_direct(1, 1)
-    ag_far(1, 1)
-    sib_start(1, 0)
-    spread(1, FC, store_up, 16, DC)
+    spread(1, FC, store_up, 0, DC)
     load(db_ref).start()
-    forward_step(0, (0,))
-    ag_forward(0, 2)
-    forward_step(1, (0,))
-    forward_step(2, (0,))
+    ag_forward(0)
+    ag_wait(1, 1)
     load(db_ref).wait()
-    spread(2, DC, store_down, 0, FC)
-    ag_direct(0, 2)
+    spread(2, DC, store_down, 0, 4)
+    ag_direct(0)
     ag_start(1, 2)
     sib_start(0, 1)
     sib_start(0, 3)
+    sib_start(1, 0)
+    spread(2, DC, store_down, 4, FC)
     pick_slots()
-    forward_step(0, (1, 3))
-    ag_far(0, 2)
+    ag_far(0)
     sib_start(0, 2)
-    forward_step(1, (1, 3))
-    ag_forward(1, 2)
-    forward_step(2, (1, 3))
-    for third in range(3):
-        forward_step(third, (2,))
-    point_forward()
-    ag_direct(1, 2)
+    forward_cols(0, 3, pl.multiple_of(mine, 512), 512)
+    ag_forward(1)
+    sib_wait(0)
+    forward_cols(0, 3, pl.multiple_of(other, 512), 512)
+    forward_cols(3, FC, 0, TOK)
+    ag_direct(1)
     sib_start(1, 1)
     sib_start(1, 3)
+    ag_far(1)
+    sib_start(1, 2)
     partial_out(0)
     rs_one(0)
-    for third in range(3):
-        backward_step(third, (0,))
+    sib_wait(1)
+
+    @pl.loop(0, 3)
+    def _(c):
+        own_backward(2 * c, 2)
+
+    own_backward(FC - 1, 1)
     rs_two(0)
-    ag_far(1, 2)
-    sib_start(1, 2)
-    for third in range(3):
-        backward_step(third, (1, 3))
-    rs_three(0)
-    for third in range(3):
-        backward_step(third, (2,))
-    point_backward()
     partial_out(1)
     rs_one(1)
-    grads(0, 3)
+    rs_three(0)
+
+    @pl.loop(0, 2)
+    def _(c):
+        backward_cols(2 * c, 2)
+
     rs_two(1)
     rs_four(0)
-    grads(3, 9)
+
+    @pl.loop(2, 3)
+    def _(c):
+        backward_cols(2 * c, 2)
+
+    backward_cols(FC - 1, 1)
     rs_three(1)
-    grads(9, 13)
+    grads(0, 10)
     rs_four(1)
-    grads(13, CAP)
+    grads(10, CAP)
     for n in range(3):
         grad_copy(n).start()
     ag_finish(0)
@@ -543,12 +502,8 @@
 
 
 def copy_body(*refs):
-    sources, targets, sem = refs[:5], refs[5:10], refs[10]
-    copies = [pltpu.make_async_copy(a, b, sem.at[n]) for n, (a, b) in enumerate(zip(sources, targets))]
-    for copy in copies:
-        copy.start()
-    for copy in copies:
-        copy.wait()
+    for source, target in zip(refs[:5], refs[5:]):
+        target[...] = source[...]
 
 
 def local(
@@ -580,14 +535,14 @@
             pltpu.SMEM((3, CAP), jnp.int32),
             pltpu.SMEM((3,), jnp.int32),
             pltpu.SMEM((3, NBLK), jnp.int32),
-            pltpu.VMEM((2, DC, 4, 4, 4, 2, 8, BLK), BF16),
+            pltpu.VMEM((2, DC, 2, 4, 4, 4, 8, BLK), BF16),
             pltpu.VMEM((FC, D, 2 * BLK), BF16),
             pltpu.VMEM((FDEV, D), BF16),
             pltpu.VMEM((KB + 1, BLK, BLK), BF16),
-            pltpu.VMEM((2 * FC, 4, 4, 4, 16, BLK), F32),
             pltpu.VMEM((FC, TOK, BLK), BF16),
             pltpu.VMEM((2 * FC, TOK, BLK), BF16),
-            pltpu.VMEM((2, 2, 4, 2, 8, D), BF16),
+            pltpu.VMEM((2 * FC, BLK, BLK), BF16),
+            pltpu.VMEM((2, 2, 2, 4, 8, D), BF16),
             pltpu.VMEM((2, 2, 4, 8, D), BF16),
             pltpu.VMEM((2, 3, 2, 8, D), BF16),
             pltpu.VMEM((2, 2, 8, D), BF16),
@@ -623,9 +578,8 @@
     lo, tg, gg, ug, dg = pl.pallas_call(
         copy_body,
         out_shape=shapes,
-        in_specs=[hbm] * 5,
-        out_specs=(hbm,) * 5,
-        scratch_shapes=[pltpu.SemaphoreType.DMA((5,))],
+        in_specs=[vmem] * 5,
+        out_specs=(vmem,) * 5,
     )(*results)
     return lo, tg, gg[None], ug[None], dg[None]
 

time: 217 us -> 101 us (0.47)
  Pallas kernels: 216 us -> 99.5 us
    pallas_call x1, Pallas kernels: 106 us -> 3.8 us  [local(): pl.pallas_call(copy_body, out_shape=shapes, in_specs=[vmem] * 5, out_spec...]
    pallas_call x1, Pallas kernels: 110 us -> 95.7 us  [local(): pl.pallas_call(kernel_body, out_shape=shapes, in_specs=[vmem, vmem] + [hb...]
where the time goes in v3:
time: 101 us; the launch traced here: 100 us
  Pallas kernels  99.5 us (99%)
    pallas_call x1, Pallas kernels, local(): pl.pallas_call(kernel_body, out_shape=shapes, in_specs=[vmem, vmem] + [hb...  95.7 us
    pallas_call x1, Pallas kernels, local(): pl.pallas_call(copy_body, out_shape=shapes, in_specs=[vmem] * 5, out_spec...  3.8 us

profile of v3, /device:TPU:0, one launch (start us, length us, event | category | flops | bytes accessed | tf_op | source)
XLA Modules:
  0.0 100.1 jit_solution(4071227340810041938)
XLA Ops:
  0.6 95.7 %shard_map.146 = (bf16[8,4096]{1,0:T(8,128)(2,1)}, bf16[8,4096]{1,0:T(8,128)(2,1)}, f32[17,128,128]{2,1,0:T(8,128)}, f32[17,128,128]{2,1,0:T(8,128)}, f32[17,128,128]{2,1,0:T(8,128)}) custom-call(bf16[8,4096]{1,0:T(8,128)(2,1)} %tok_ref.1, bf16[8,4096]{1,0:T(8,128)(2,1)} %cot_ref.1, bf16[112,128,128]{2,1,0:T(8,128)(2,1)} %gb_ref.1, ...), custom_call_target="tpu_custom_call" | custom-call | tf_op jit(solution)/shard_map/pallas_call | solution.py:527
  96.3 3.8 %shard_map.147 = (bf16[8,4096]{1,0:T(8,128)(2,1)}, bf16[8,4096]{1,0:T(8,128)(2,1)}, f32[17,128,128]{2,1,0:T(8,128)}, f32[17,128,128]{2,1,0:T(8,128)}, f32[17,128,128]{2,1,0:T(8,128)}) custom-call(bf16[8,4096]{1,0:T(8,128)(2,1)} %get-tuple-element.15.refs_0_, bf16[8,4096]{1,0:T(8,128)(2,1)} %get-tuple-element.16.refs_1_, ...), custom_call_target="tpu_custom_call" | custom-call | tf_op jit(solution)/shard_map/pallas_call | solution.py:578

commit v4 on v3

--- a/solution.py
+++ b/solution.py
@@ -66,11 +66,8 @@
     got2,
     mid,
     got3,
-    rows_out,
-    grad_out,
     in_sem,
     ld_sem,
-    out_sem,
     ag_send,
     ag_recv,
     sib_send,
@@ -265,7 +262,7 @@
     def rows_of(q, rows):
         return jnp.concatenate([flat[q, j, rows, :] for j in range(DC)], axis=1)
 
-    def forward_cols(lo, hi, start, size):
+    def forward_cols(lo, hi, start, size, then):
         @pl.loop(lo, hi)
         def _(c):
             for rows in [pl.ds(start, size)]:
@@ -276,6 +273,9 @@
                 hid[c, rows, :] = (swish * up).astype(BF16)
                 gpre[2 * c, rows, :] = (up * sigma * (1.0 + gate * (1.0 - sigma))).astype(BF16)
                 gpre[2 * c + 1, rows, :] = swish.astype(BF16)
+
+            for last, step in then.items():
+                pl.when(c == last)(step)
 
     def backward_cols(start, width):
         for rows in [pl.ds(0, TOK)]:
@@ -375,13 +375,10 @@
             mid[o, h] = total.astype(BF16)
         rs_copy(o, 4).start()
 
-    def row_copy(o):
-        return pltpu.make_async_copy(rows_out.at[o], (lo_ref, tg_ref)[o], out_sem.at[o])
-
     def rs_four(o):
         rs_copy(o, 4).wait_recv()
-        rows_out[o] = (mid[o, yhi].astype(F32) + got3[o].astype(F32)).astype(BF16)
-        row_copy(o).start()
+        total = mid[o, yhi].astype(F32) + got3[o].astype(F32)
+        (lo_ref, tg_ref)[o][...] = total.astype(BF16)
         for k in range(5):
             rs_copy(o, k).wait_send()
 
@@ -413,37 +410,34 @@
                 else:
                     left = hid[block // DC]
                     right = buf[1, block % DC].reshape(TOK, BLK)
-                grad_out[n, v] = block_grad(left, right, weight)
-
-    def grad_copy(n):
-        return pltpu.make_async_copy(grad_out.at[n], (gg_ref, ug_ref, dg_ref)[n], out_sem.at[2 + n])
+                (gg_ref, ug_ref, dg_ref)[n][v] = block_grad(left, right, weight)
 
     mine, other = core * 512, (1 - core) * 512
     ag_start(0, 0)
+    ag_start(1, 0)
     stage[KB] = jnp.zeros((BLK, BLK), BF16)
     for copy in small:
         copy.wait()
     find_blocks()
     ag_wait(0, 0)
     ag_start(0, 1)
-    ag_start(1, 0)
+    ag_wait(1, 0)
+    ag_start(1, 1)
     load(gb_ref).wait()
     spread(0, FC, store_gate, 0, DC)
     load(ub_ref).start()
     ag_wait(0, 1)
     ag_start(0, 2)
-    ag_wait(1, 0)
-    ag_start(1, 1)
+    ag_wait(1, 1)
     sib_start(0, 0)
     load(ub_ref).wait()
     spread(1, FC, store_up, 0, DC)
     load(db_ref).start()
     ag_forward(0)
-    ag_wait(1, 1)
+    ag_start(1, 2)
     load(db_ref).wait()
     spread(2, DC, store_down, 0, 4)
     ag_direct(0)
-    ag_start(1, 2)
     sib_start(0, 1)
     sib_start(0, 3)
     sib_start(1, 0)
@@ -451,16 +445,21 @@
     pick_slots()
     ag_far(0)
     sib_start(0, 2)
-    forward_cols(0, 3, pl.multiple_of(mine, 512), 512)
+    forward_cols(0, 3, pl.multiple_of(mine, 512), 512, {})
     ag_forward(1)
     sib_wait(0)
-    forward_cols(0, 3, pl.multiple_of(other, 512), 512)
-    forward_cols(3, FC, 0, TOK)
-    ag_direct(1)
-    sib_start(1, 1)
-    sib_start(1, 3)
-    ag_far(1)
-    sib_start(1, 2)
+    forward_cols(0, 3, pl.multiple_of(other, 512), 512, {})
+
+    def cots_direct():
+        ag_direct(1)
+        sib_start(1, 1)
+        sib_start(1, 3)
+
+    def cots_far():
+        ag_far(1)
+        sib_start(1, 2)
+
+    forward_cols(3, FC, 0, TOK, {3: cots_direct, 5: cots_far})
     partial_out(0)
     rs_one(0)
     sib_wait(1)
@@ -470,40 +469,39 @@
         own_backward(2 * c, 2)
 
     own_backward(FC - 1, 1)
+    partial_out(1)
     rs_two(0)
-    partial_out(1)
     rs_one(1)
-    rs_three(0)
-
-    @pl.loop(0, 2)
+
+    @pl.loop(0, 3)
     def _(c):
         backward_cols(2 * c, 2)
 
-    rs_two(1)
+        @pl.when(c == 1)
+        def _():
+            rs_two(1)
+
+    rs_three(0)
+    backward_cols(FC - 1, 1)
+    grads(0, 7)
+    rs_three(1)
     rs_four(0)
-
-    @pl.loop(2, 3)
-    def _(c):
-        backward_cols(2 * c, 2)
-
-    backward_cols(FC - 1, 1)
-    rs_three(1)
-    grads(0, 10)
+    grads(7, CAP)
     rs_four(1)
-    grads(10, CAP)
-    for n in range(3):
-        grad_copy(n).start()
     ag_finish(0)
     ag_finish(1)
-    for o in range(2):
-        row_copy(o).wait()
-    for n in range(3):
-        grad_copy(n).wait()
 
 
 def copy_body(*refs):
-    for source, target in zip(refs[:5], refs[5:]):
-        target[...] = source[...]
+    sem = refs[10]
+    copies = [
+        pltpu.make_async_copy(source, target, sem.at[n])
+        for n, (source, target) in enumerate(zip(refs[:5], refs[5:10]))
+    ]
+    for copy in copies:
+        copy.start()
+    for copy in copies:
+        copy.wait()
 
 
 def local(
@@ -526,9 +524,9 @@
     shapes = (rows, rows, owned, owned, owned)
     results = pl.pallas_call(
         kernel_body,
-        out_shape=shapes,
+        out_shape=tuple(pltpu.VMEM(shape.shape, shape.dtype) for shape in shapes),
         in_specs=[vmem, vmem] + [hbm] * 9,
-        out_specs=(hbm,) * 5,
+        out_specs=(vmem,) * 5,
         scratch_shapes=[pltpu.SMEM((1, KB), jnp.int32)] * 3
         + [pltpu.VMEM((1, KB), jnp.int32)] * 6
         + [
@@ -547,11 +545,8 @@
             pltpu.VMEM((2, 3, 2, 8, D), BF16),
             pltpu.VMEM((2, 2, 8, D), BF16),
             pltpu.VMEM((2, 8, D), BF16),
-            pltpu.VMEM((2, 8, D), BF16),
-            pltpu.VMEM((3, CAP, BLK, BLK), F32),
             pltpu.SemaphoreType.DMA((9,)),
             pltpu.SemaphoreType.DMA,
-            pltpu.SemaphoreType.DMA((5,)),
             pltpu.SemaphoreType.DMA((2, 3, 3, 6)),
             pltpu.SemaphoreType.DMA((2, 3, 3, 6)),
             pltpu.SemaphoreType.DMA((2, 3, 4)),
@@ -560,7 +555,7 @@
             pltpu.SemaphoreType.DMA((2, 5)),
         ],
         compiler_params=pltpu.CompilerParams(
-            collective_id=0, has_side_effects=True, vmem_limit_bytes=62 * 1024 * 1024
+            collective_id=0, has_side_effects=True, vmem_limit_bytes=56 * 1024 * 1024
         ),
     )(
         tokens,
@@ -579,7 +574,8 @@
         copy_body,
         out_shape=shapes,
         in_specs=[vmem] * 5,
-        out_specs=(vmem,) * 5,
+        out_specs=(hbm,) * 5,
+        scratch_shapes=[pltpu.SemaphoreType.DMA((5,))],
     )(*results)
     return lo, tg, gg[None], ug[None], dg[None]
 

time: 101 us -> 95.1 us (0.942)
  Pallas kernels: 99.5 us -> 89.9 us
  local copies, waits for them, and re-layouts: 0 us -> 4.29 us
    pallas_call x1, Pallas kernels: 95.7 us -> 86.1 us  [local(): pl.pallas_call(kernel_body, out_shape=tuple((pltpu.VMEM(shape.shape, shap...]
    unnamed x0 -> x10, local copies, waits for them, and re-layouts: none -> 4.29 us
where the time goes in v4:
time: 95.1 us; the launch traced here: 94.9 us
  Pallas kernels  89.9 us (95%)
  local copies, waits for them, and re-layouts  4.29 us (5%)
    pallas_call x1, Pallas kernels, local(): pl.pallas_call(kernel_body, out_shape=tuple((pltpu.VMEM(shape.shape, shap...  86.1 us
    unnamed x10, local copies, waits for them, and re-layouts  4.29 us
    pallas_call x1, Pallas kernels, local(): pl.pallas_call(copy_body, out_shape=shapes, in_specs=[vmem] * 5, out_spec...  3.78 us

profile of v4, /device:TPU:0, one launch (start us, length us, event | category | flops | bytes accessed | tf_op | source)
XLA Modules:
  0.0 94.9 jit_solution(12668280583248290492)
XLA Ops:
  0.6 86.1 %shard_map.146 = (bf16[8,4096]{1,0:T(8,128)(2,1)S(1)}, bf16[8,4096]{1,0:T(8,128)(2,1)S(1)}, f32[17,128,128]{2,1,0:T(8,128)S(1)}, f32[17,128,128]{2,1,0:T(8,128)S(1)}, f32[17,128,128]{2,1,0:T(8,128)S(1)}) custom-call(bf16[8,4096]{1,0:T(8,128)(2,1)} %tok_ref.1, bf16[8,4096]{1,0:T(8,128)(2,1)} %cot_ref.1, bf16[112,128,128]{2,1,0:T(8,128)(2,1)} %gb_ref.1, ...), custom_call_target="tpu_custom_call" | custom-call | tf_op jit(solution)/shard_map/pallas_call | solution.py:525
  86.8 0.0 copy-start
  86.8 1.0 %copy-done = f32[17,128,128]{2,1,0:T(8,128)} copy-done((f32[17,128,128]{2,1,0:T(8,128)}, f32[17,128,128]{2,1,0:T(8,128)S(1)}, u32[]{:S(2)}) %copy-start) | copy-done | bytes 1114136
  87.8 0.0 copy-start.1
  87.8 1.0 %copy-done.1 = f32[17,128,128]{2,1,0:T(8,128)} copy-done((f32[17,128,128]{2,1,0:T(8,128)}, f32[17,128,128]{2,1,0:T(8,128)S(1)}, u32[]{:S(2)}) %copy-start.1) | copy-done | bytes 1114136
  88.8 0.0 copy-start.2
  88.8 1.0 %copy-done.2 = f32[17,128,128]{2,1,0:T(8,128)} copy-done((f32[17,128,128]{2,1,0:T(8,128)}, f32[17,128,128]{2,1,0:T(8,128)S(1)}, u32[]{:S(2)}) %copy-start.2) | copy-done | bytes 1114136
  89.8 0.0 copy-start.3
  89.8 0.6 copy-done.3
  90.5 0.0 copy-start.4
  90.5 0.6 copy-done.4
  91.1 3.8 %shard_map.147 = (bf16[8,4096]{1,0:T(8,128)(2,1)}, bf16[8,4096]{1,0:T(8,128)(2,1)}, f32[17,128,128]{2,1,0:T(8,128)}, f32[17,128,128]{2,1,0:T(8,128)}, f32[17,128,128]{2,1,0:T(8,128)}) custom-call(bf16[8,4096]{1,0:T(8,128)(2,1)} %copy-done.3, bf16[8,4096]{1,0:T(8,128)(2,1)} %copy-done.4, f32[17,128,128]{2,1,0:T(8,128)} %copy-done, f32[17,128,128]{2,1,0:T(8,128)} %copy-done.1, ...), custom_call_target="tpu_custom_call" | custom-call | tf_op jit(solution)/shard_map/pallas_call | solution.py:573
Async XLA Ops:
  86.8 1.0 %copy-start = (f32[17,128,128]{2,1,0:T(8,128)}, f32[17,128,128]{2,1,0:T(8,128)S(1)}, u32[]{:S(2)}) copy-start(f32[17,128,128]{2,1,0:T(8,128)S(1)} %get-tuple-element.17.refs_2_) | copy-start | bytes 3342340
  87.8 1.0 %copy-start.1 = (f32[17,128,128]{2,1,0:T(8,128)}, f32[17,128,128]{2,1,0:T(8,128)S(1)}, u32[]{:S(2)}) copy-start(f32[17,128,128]{2,1,0:T(8,128)S(1)} %get-tuple-element.18.refs_3_) | copy-start | bytes 3342340
  88.8 1.0 %copy-start.2 = (f32[17,128,128]{2,1,0:T(8,128)}, f32[17,128,128]{2,1,0:T(8,128)S(1)}, u32[]{:S(2)}) copy-start(f32[17,128,128]{2,1,0:T(8,128)S(1)} %get-tuple-element.19.refs_4_) | copy-start | bytes 3342340
  89.8 0.6 copy-start.3
  90.5 0.6 copy-start.4

commit v5 on v4

--- a/solution.py
+++ b/solution.py
@@ -576,7 +576,7 @@
         in_specs=[vmem] * 5,
         out_specs=(hbm,) * 5,
         scratch_shapes=[pltpu.SemaphoreType.DMA((5,))],
-    )(*results)
+    )(*[pltpu.with_memory_space_constraint(r, pltpu.VMEM) for r in results])
     return lo, tg, gg[None], ug[None], dg[None]
 
 

time: 95.1 us -> 88.8 us (0.934)
  local copies, waits for them, and re-layouts: 4.29 us -> 0 us
  Pallas kernels: 89.9 us -> 88 us
    unnamed x10 -> x0, local copies, waits for them, and re-layouts: 4.29 us -> none
    pallas_call x1, Pallas kernels: 3.78 us -> 1.81 us  [local(): pl.pallas_call(copy_body, out_shape=shapes, in_specs=[vmem] * 5, out_spec...]
where the time goes in v5:
time: 88.8 us; the launch traced here: 88.6 us
  Pallas kernels  88 us (99%)
    pallas_call x1, Pallas kernels, local(): pl.pallas_call(kernel_body, out_shape=tuple((pltpu.VMEM(shape.shape, shap...  86.1 us
    pallas_call x1, Pallas kernels, local(): pl.pallas_call(copy_body, out_shape=shapes, in_specs=[vmem] * 5, out_spec...  1.81 us

profile of v5, /device:TPU:0, one launch (start us, length us, event | category | flops | bytes accessed | tf_op | source)
XLA Modules:
  0.0 88.6 jit_solution(5148781264748040354)
XLA Ops:
  0.6 86.1 %shard_map.146 = (bf16[8,4096]{1,0:T(8,128)(2,1)S(1)}, bf16[8,4096]{1,0:T(8,128)(2,1)S(1)}, f32[17,128,128]{2,1,0:T(8,128)S(1)}, f32[17,128,128]{2,1,0:T(8,128)S(1)}, f32[17,128,128]{2,1,0:T(8,128)S(1)}) custom-call(bf16[8,4096]{1,0:T(8,128)(2,1)} %tok_ref.1, bf16[8,4096]{1,0:T(8,128)(2,1)} %cot_ref.1, bf16[112,128,128]{2,1,0:T(8,128)(2,1)} %gb_ref.1, ...), custom_call_target="tpu_custom_call" | custom-call | tf_op jit(solution)/shard_map/pallas_call | solution.py:525
  86.8 1.8 %shard_map.147 = (bf16[8,4096]{1,0:T(8,128)(2,1)}, bf16[8,4096]{1,0:T(8,128)(2,1)}, f32[17,128,128]{2,1,0:T(8,128)}, f32[17,128,128]{2,1,0:T(8,128)}, f32[17,128,128]{2,1,0:T(8,128)}) custom-call(bf16[8,4096]{1,0:T(8,128)(2,1)S(1)} %get-tuple-element.15.refs_0_, bf16[8,4096]{1,0:T(8,128)(2,1)S(1)} %get-tuple-element.16.refs_1_, ...), custom_call_target="tpu_custom_call" | custom-call | tf_op jit(solution)/shard_map/pallas_call | solution.py:573

commit v6 on v5

--- a/solution.py
+++ b/solution.py
@@ -21,7 +21,8 @@
 F32 = jnp.float32
 BF16 = jnp.bfloat16
 
-THIRDS = ((0, 6, 12), (12, 17, 22), (22, 27, 32))
+THIRDS = ((0, 6, 11), (11, 16, 22), (22, 27, 32))
+RELAYED = ((0, 2), (1, 1), (1, 2))
 ORDERS = (("x", "y", "z"), ("y", "z", "x"), ("z", "x", "y"))
 
 
@@ -147,7 +148,7 @@
         lo, mid_col, hi = THIRDS[third]
         axis = ORDERS[third][phase]
         own = here[axis]
-        if phase < 2:
+        if (q, phase) not in RELAYED:
             along, cols, to = own, (lo, hi), (right, left, far)[k]
         else:
             along, cols, to = (
@@ -182,7 +183,7 @@
         )
 
     def ag_start(q, phase):
-        for k in range(4 if phase == 2 else 3):
+        for k in range(4 if (q, phase) in RELAYED else 3):
             for third in range(3):
                 ag_copy(q, third, phase, k).start()
 
@@ -191,22 +192,22 @@
             for k in range(3):
                 ag_copy(q, third, phase, k).wait_recv()
 
-    def ag_forward(q):
+    def ag_forward(q, phase=2):
         for third in range(3):
-            ag_copy(q, third, 2, 0).wait_recv()
-            ag_copy(q, third, 2, 4).start()
-            ag_copy(q, third, 2, 1).wait_recv()
-            ag_copy(q, third, 2, 5).start()
-
-    def ag_direct(q):
+            ag_copy(q, third, phase, 0).wait_recv()
+            ag_copy(q, third, phase, 4).start()
+            ag_copy(q, third, phase, 1).wait_recv()
+            ag_copy(q, third, phase, 5).start()
+
+    def ag_direct(q, phase=2):
         for third in range(3):
-            ag_copy(q, third, 2, 2).wait_recv()
-            ag_copy(q, third, 2, 3).wait_recv()
-
-    def ag_far(q):
+            ag_copy(q, third, phase, 2).wait_recv()
+            ag_copy(q, third, phase, 3).wait_recv()
+
+    def ag_far(q, phase=2):
         for third in range(3):
-            ag_copy(q, third, 2, 4).wait_recv()
-            ag_copy(q, third, 2, 5).wait_recv()
+            ag_copy(q, third, phase, 4).wait_recv()
+            ag_copy(q, third, phase, 5).wait_recv()
 
     def sib_start(q, k):
         for third in range(3):
@@ -220,7 +221,7 @@
     def ag_finish(q):
         for third in range(3):
             for phase in range(3):
-                for k in range(6 if phase == 2 else 3):
+                for k in range(6 if (q, phase) in RELAYED else 3):
                     ag_copy(q, third, phase, k).wait_send()
             for k in range(4):
                 sib_copy(q, third, k).wait_send()
@@ -428,12 +429,14 @@
     load(ub_ref).start()
     ag_wait(0, 1)
     ag_start(0, 2)
-    ag_wait(1, 1)
     sib_start(0, 0)
+    ag_forward(1, 1)
     load(ub_ref).wait()
     spread(1, FC, store_up, 0, DC)
     load(db_ref).start()
     ag_forward(0)
+    ag_direct(1, 1)
+    ag_far(1, 1)
     ag_start(1, 2)
     load(db_ref).wait()
     spread(2, DC, store_down, 0, 4)

time: 88.8 us -> 87.5 us (0.985)
  Pallas kernels: 88 us -> 86.6 us
    pallas_call x1, Pallas kernels: 86.1 us -> 84.8 us  [local(): pl.pallas_call(kernel_body, out_shape=tuple((pltpu.VMEM(shape.shape, shap...]
where the time goes in v6:
time: 87.5 us; the launch traced here: 87.2 us
  Pallas kernels  86.6 us (99%)
    pallas_call x1, Pallas kernels, local(): pl.pallas_call(kernel_body, out_shape=tuple((pltpu.VMEM(shape.shape, shap...  84.8 us
    pallas_call x1, Pallas kernels, local(): pl.pallas_call(copy_body, out_shape=shapes, in_specs=[vmem] * 5, out_spec...  1.81 us

profile of v6, /device:TPU:0, one launch (start us, length us, event | category | flops | bytes accessed | tf_op | source)
XLA Modules:
  0.0 87.2 jit_solution(12523874572424813616)
XLA Ops:
  0.6 84.8 %shard_map.146 = (bf16[8,4096]{1,0:T(8,128)(2,1)S(1)}, bf16[8,4096]{1,0:T(8,128)(2,1)S(1)}, f32[17,128,128]{2,1,0:T(8,128)S(1)}, f32[17,128,128]{2,1,0:T(8,128)S(1)}, f32[17,128,128]{2,1,0:T(8,128)S(1)}) custom-call(bf16[8,4096]{1,0:T(8,128)(2,1)} %tok_ref.1, bf16[8,4096]{1,0:T(8,128)(2,1)} %cot_ref.1, bf16[112,128,128]{2,1,0:T(8,128)(2,1)} %gb_ref.1, ...), custom_call_target="tpu_custom_call" | custom-call | tf_op jit(solution)/shard_map/pallas_call | solution.py:528
  85.4 1.8 %shard_map.147 = (bf16[8,4096]{1,0:T(8,128)(2,1)}, bf16[8,4096]{1,0:T(8,128)(2,1)}, f32[17,128,128]{2,1,0:T(8,128)}, f32[17,128,128]{2,1,0:T(8,128)}, f32[17,128,128]{2,1,0:T(8,128)}) custom-call(bf16[8,4096]{1,0:T(8,128)(2,1)S(1)} %get-tuple-element.15.refs_0_, bf16[8,4096]{1,0:T(8,128)(2,1)S(1)} %get-tuple-element.16.refs_1_, ...), custom_call_target="tpu_custom_call" | custom-call | tf_op jit(solution)/shard_map/pallas_call | solution.py:576

commit v7 on v6

--- a/solution.py
+++ b/solution.py
@@ -187,11 +187,6 @@
             for third in range(3):
                 ag_copy(q, third, phase, k).start()
 
-    def ag_wait(q, phase):
-        for third in range(3):
-            for k in range(3):
-                ag_copy(q, third, phase, k).wait_recv()
-
     def ag_forward(q, phase=2):
         for third in range(3):
             ag_copy(q, third, phase, 0).wait_recv()
@@ -208,6 +203,26 @@
         for third in range(3):
             ag_copy(q, third, phase, 4).wait_recv()
             ag_copy(q, third, phase, 5).wait_recv()
+
+    def ag_next(q, phase):
+        for third in range(3):
+            for k in range(3):
+                ag_copy(q, third, phase, k).wait_recv()
+            for k in range(4 if (q, phase + 1) in RELAYED else 3):
+                ag_copy(q, third, phase + 1, k).start()
+
+    def ag_last(q):
+        for third in range(3):
+            ag_copy(q, third, 2, 4).wait_recv()
+            ag_copy(q, third, 2, 5).wait_recv()
+            sib_copy(q, third, 2).start()
+
+    def ag_sides(q):
+        for third in range(3):
+            ag_copy(q, third, 2, 2).wait_recv()
+            ag_copy(q, third, 2, 3).wait_recv()
+            sib_copy(q, third, 1).start()
+            sib_copy(q, third, 3).start()
 
     def sib_start(q, k):
         for third in range(3):
@@ -320,7 +335,7 @@
                 own_g[k] = (slope * piece).astype(BF16)
 
     def partial_out(o):
-        width = 512
+        width = 1024
 
         @pl.loop(0, D // width)
         def _(n):
@@ -420,15 +435,12 @@
     for copy in small:
         copy.wait()
     find_blocks()
-    ag_wait(0, 0)
-    ag_start(0, 1)
-    ag_wait(1, 0)
-    ag_start(1, 1)
+    ag_next(0, 0)
+    ag_next(1, 0)
     load(gb_ref).wait()
     spread(0, FC, store_gate, 0, DC)
     load(ub_ref).start()
-    ag_wait(0, 1)
-    ag_start(0, 2)
+    ag_next(0, 1)
     sib_start(0, 0)
     ag_forward(1, 1)
     load(ub_ref).wait()
@@ -440,27 +452,21 @@
     ag_start(1, 2)
     load(db_ref).wait()
     spread(2, DC, store_down, 0, 4)
-    ag_direct(0)
-    sib_start(0, 1)
-    sib_start(0, 3)
+    ag_sides(0)
     sib_start(1, 0)
     spread(2, DC, store_down, 4, FC)
     pick_slots()
-    ag_far(0)
-    sib_start(0, 2)
+    ag_last(0)
     forward_cols(0, 3, pl.multiple_of(mine, 512), 512, {})
     ag_forward(1)
     sib_wait(0)
     forward_cols(0, 3, pl.multiple_of(other, 512), 512, {})
 
     def cots_direct():
-        ag_direct(1)
-        sib_start(1, 1)
-        sib_start(1, 3)
+        ag_sides(1)
 
     def cots_far():
-        ag_far(1)
-        sib_start(1, 2)
+        ag_last(1)
 
     forward_cols(3, FC, 0, TOK, {3: cots_direct, 5: cots_far})
     partial_out(0)

time: 87.5 us -> 86.6 us (0.990)
  Pallas kernels: 86.6 us -> 84.9 us
    pallas_call x1, Pallas kernels: 84.8 us -> 83.1 us  [local(): pl.pallas_call(kernel_body, out_shape=tuple((pltpu.VMEM(shape.shape, shap...]
where the time goes in v7:
time: 86.6 us; the launch traced here: 85.6 us
  Pallas kernels  84.9 us (98%)
    pallas_call x1, Pallas kernels, local(): pl.pallas_call(kernel_body, out_shape=tuple((pltpu.VMEM(shape.shape, shap...  83.1 us
    pallas_call x1, Pallas kernels, local(): pl.pallas_call(copy_body, out_shape=shapes, in_specs=[vmem] * 5, out_spec...  1.81 us

profile of v7, /device:TPU:0, one launch (start us, length us, event | category | flops | bytes accessed | tf_op | source)
XLA Modules:
  0.0 85.6 jit_solution(3490625749349586735)
XLA Ops:
  0.6 83.1 %shard_map.146 = (bf16[8,4096]{1,0:T(8,128)(2,1)S(1)}, bf16[8,4096]{1,0:T(8,128)(2,1)S(1)}, f32[17,128,128]{2,1,0:T(8,128)S(1)}, f32[17,128,128]{2,1,0:T(8,128)S(1)}, f32[17,128,128]{2,1,0:T(8,128)S(1)}) custom-call(bf16[8,4096]{1,0:T(8,128)(2,1)} %tok_ref.1, bf16[8,4096]{1,0:T(8,128)(2,1)} %cot_ref.1, bf16[112,128,128]{2,1,0:T(8,128)(2,1)} %gb_ref.1, ...), custom_call_target="tpu_custom_call" | custom-call | tf_op jit(solution)/shard_map/pallas_call | solution.py:534
  83.8 1.8 %shard_map.147 = (bf16[8,4096]{1,0:T(8,128)(2,1)}, bf16[8,4096]{1,0:T(8,128)(2,1)}, f32[17,128,128]{2,1,0:T(8,128)}, f32[17,128,128]{2,1,0:T(8,128)}, f32[17,128,128]{2,1,0:T(8,128)}) custom-call(bf16[8,4096]{1,0:T(8,128)(2,1)S(1)} %get-tuple-element.15.refs_0_, bf16[8,4096]{1,0:T(8,128)(2,1)S(1)} %get-tuple-element.16.refs_1_, ...), custom_call_target="tpu_custom_call" | custom-call | tf_op jit(solution)/shard_map/pallas_call | solution.py:582
